TPU v7x, 512 devices: a whole 4x4x16 slice. The times are simulated.
512 devices in a mesh: depth: 8 (over z_hi, core), scan: 64 (over z_lo, y, x).
Axes of the slice: x: 4, y: 4, z: 16 (z_hi: 4, z_lo: 4; z = z_hi * 4 + z_lo), core: 2. Of those that a mesh axis runs over, the one named last changes fastest.
Arguments:
- objects: float32 [24, 2, 8192, 256], P('depth', None, 'scan')
- probe: float32 [2, 128, 128], replicated, may hold values from -6 to 6
- row_offsets: int32 [128], P('scan'), may hold values from 0 to 8192, as said below
- col_offsets: int32 [128], P('scan'), may hold values from 0 to 128, as said below
- intensity: float32 [128, 128, 128], P('scan'), may hold values from 0.1 to 4
Outputs:
- object_grad: float32 [24, 2, 8192, 256], P('depth', None, 'scan')
- probe_grad: float32 [2, 128, 128], P(None, 'depth')
Inputs may be any that keep to these rules, and one draw needn't show every extreme that they name: `row_offsets`: position i is measured by scan index i // 2; its row offset lies from (i // 2) * 128 to (i // 2 + 1) * 128, both ends included, and on every scan index one of its positions has the upper end. `col_offsets`: some position has column offset 0 and some has the largest.
All inputs are finite; a program needn't handle non-finite values.
Results may differ from a plain program's by a relative error of at most 0.0003.
Values sent between devices are 32-bit elements; how exact they have to be, the bound alone decides.
A program may use at most 64 MiB of HBM per device.

v0:
```python
import math

import jax
import jax.numpy as jnp
from jax import lax
from jax.sharding import PartitionSpec as P

PROPAGATION = 0.5


def from_behind(block, axis, distance):
    devices = range(lax.axis_size(axis))
    route = [((i - distance) % len(devices), i) for i in devices]
    return lax.ppermute(block, axis, route)


def passed_along(block, axis, distance):
    devices = range(lax.axis_size(axis))
    route = [(i - distance, i) for i in devices if i - distance in devices]
    return lax.ppermute(block, axis, route)


def broadcast(x, axis, root):
    mine = lax.axis_index(axis) == root
    return lax.psum(jnp.where(mine, x, jnp.zeros_like(x)), axis)


def matmul_high(left_side, right_side):
    return jnp.matmul(left_side, right_side, precision=lax.Precision.HIGHEST)


def dft_tables(window_width):
    grid_index = jnp.arange(window_width, dtype=jnp.int32)
    phase_steps = grid_index[:, None] * grid_index[None, :] % window_width
    turn_angle = phase_steps.astype(jnp.float32) * (2.0 * math.pi / window_width)
    norm_scale = 1.0 / math.sqrt(window_width)
    return (jnp.cos(turn_angle) * norm_scale, jnp.sin(turn_angle) * norm_scale)


def chirp_factors(window_width):
    grid_index = jnp.arange(window_width, dtype=jnp.int32)
    frequency = jnp.where(grid_index < window_width // 2, grid_index, grid_index - window_width)
    squared = frequency[:, None] ** 2 + frequency[None, :] ** 2
    phase_angle = squared.astype(jnp.float32) * (PROPAGATION * math.pi / window_width)
    return (jnp.cos(phase_angle), jnp.sin(phase_angle))


def transform(real_part, imag_part, tables, direction):
    cos_table, sin_table = tables
    mid_real = matmul_high(cos_table, real_part) + direction * matmul_high(sin_table, imag_part)
    mid_imag = matmul_high(cos_table, imag_part) - direction * matmul_high(sin_table, real_part)
    out_real = matmul_high(mid_real, cos_table) + direction * matmul_high(mid_imag, sin_table)
    out_imag = matmul_high(mid_imag, cos_table) - direction * matmul_high(mid_real, sin_table)
    return (out_real, out_imag)


def propagate(real_part, imag_part, tables, chirp_table, direction):
    chirp_cos, chirp_sin = chirp_table
    spec_real, spec_imag = transform(real_part, imag_part, tables, 1.0)
    next_real = spec_real * chirp_cos + direction * spec_imag * chirp_sin
    next_imag = spec_imag * chirp_cos - direction * spec_real * chirp_sin
    return transform(next_real, next_imag, tables, -1.0)


def forward_section(wave, patches, tables, chirp_table):
    wave_real, wave_imag = (wave[0], wave[1])
    inputs = []
    for layer_index in range(patches.shape[0]):
        inputs.append(jnp.stack([wave_real, wave_imag]))
        obj_real, obj_imag = (patches[layer_index, 0], patches[layer_index, 1])
        exit_real = wave_real * obj_real - wave_imag * obj_imag
        exit_imag = wave_real * obj_imag + wave_imag * obj_real
        wave_real, wave_imag = propagate(exit_real, exit_imag, tables, chirp_table, 1.0)
    return (jnp.stack([wave_real, wave_imag]), jnp.stack(inputs))


def backward_section(gradient, patches, inputs, tables, chirp_table):
    grad_real, grad_imag = (gradient[0], gradient[1])
    patch_grads = [None] * patches.shape[0]
    for layer_index in reversed(range(patches.shape[0])):
        chi_real, chi_imag = propagate(grad_real, grad_imag, tables, chirp_table, -1.0)
        psi_real, psi_imag = (inputs[layer_index, 0], inputs[layer_index, 1])
        patch_grads[layer_index] = jnp.stack(
            [psi_real * chi_real + psi_imag * chi_imag, psi_real * chi_imag - psi_imag * chi_real]
        )
        obj_real, obj_imag = (patches[layer_index, 0], patches[layer_index, 1])
        grad_real = obj_real * chi_real + obj_imag * chi_imag
        grad_imag = obj_real * chi_imag - obj_imag * chi_real
    return (jnp.stack([grad_real, grad_imag]), jnp.stack(patch_grads))


def far_field(exit_wave, measured, tables):
    far_real, far_imag = transform(exit_wave[0], exit_wave[1], tables, 1.0)
    misfit = far_real * far_real + far_imag * far_imag - measured
    back_real, back_imag = transform(2.0 * misfit * far_real, 2.0 * misfit * far_imag, tables, -1.0)
    return jnp.stack([back_real, back_imag])


def body(objects, probe, row_offsets, col_offsets, intensity):
    slab_count = objects.shape[0]
    tile_rows = objects.shape[2]
    window_width = probe.shape[-1]
    wave_count = row_offsets.shape[0]
    depth_count = lax.axis_size("depth")
    depth_index = lax.axis_index("depth")
    scan_index = lax.axis_index("scan")
    first_section = depth_index == 0
    last_section = depth_index == depth_count - 1
    tables = dft_tables(window_width)
    chirp_table = chirp_factors(window_width)
    local_rows = row_offsets - scan_index * tile_rows
    window_shape = (slab_count, 2, window_width, window_width)
    probe_rows = window_width // depth_count
    row_start = depth_index * probe_rows
    below_rows = from_behind(objects, "scan", -1)
    extended = jnp.concatenate([objects, below_rows], axis=2)

    def window_at(wave_index):
        return lax.dynamic_slice(
            extended, (0, 0, local_rows[wave_index], col_offsets[wave_index]), window_shape
        )

    def add_window(accum, wave_index, update):
        corner = (0, 0, local_rows[wave_index], col_offsets[wave_index])
        return lax.dynamic_update_slice(
            accum, lax.dynamic_slice(accum, corner, window_shape) + update, corner
        )

    accum_start = jnp.zeros(extended.shape, jnp.float32)
    empty_wave = jnp.zeros((2, window_width, window_width), jnp.float32)
    stored_start = jnp.zeros((wave_count,) + window_shape, jnp.float32)
    exits_start = jnp.zeros((wave_count, 2, window_width, window_width), jnp.float32)
    probe_start = jnp.zeros(probe.shape, jnp.float32)

    def forward_step(step_index, loop_state):
        outgoing, stored, exits = loop_state
        arriving = passed_along(outgoing, "depth", 1)
        arriving = jnp.where(first_section, probe, arriving)
        wave_index = step_index - depth_index
        active_step = (wave_index >= 0) & (wave_index < wave_count)
        chosen = jnp.clip(wave_index, 0, wave_count - 1)

        def forward_run_section(operand):
            leaving, inputs = forward_section(arriving, window_at(chosen), tables, chirp_table)
            return (
                leaving,
                lax.dynamic_update_index_in_dim(stored, inputs, chosen, 0),
                lax.dynamic_update_index_in_dim(exits, leaving, chosen, 0),
            )

        def forward_pass_along(operand):
            return (empty_wave, stored, exits)

        return lax.cond(active_step, forward_run_section, forward_pass_along, 0)

    outgoing, stored, exits = lax.fori_loop(
        0, wave_count + depth_count - 1, forward_step, (empty_wave, stored_start, exits_start)
    )

    def backward_step(step_index, loop_state):
        outgoing, accum, probe_part = loop_state
        arriving = passed_along(outgoing, "depth", -1)
        wave_index = step_index - (depth_count - 1 - depth_index)
        active_step = (wave_index >= 0) & (wave_index < wave_count)
        chosen = jnp.clip(wave_index, 0, wave_count - 1)

        def backward_run_section(operand):

            def from_detector(inner):
                return far_field(exits[chosen], intensity[chosen], tables)

            def from_next(inner):
                return arriving

            incoming = lax.cond(last_section, from_detector, from_next, 0)
            leaving, patch_grads = backward_section(
                incoming, window_at(chosen), stored[chosen], tables, chirp_table
            )
            return (
                leaving,
                add_window(accum, chosen, patch_grads),
                probe_part + jnp.where(first_section, leaving, 0.0),
            )

        def backward_pass_along(operand):
            return (empty_wave, accum, probe_part)

        return lax.cond(active_step, backward_run_section, backward_pass_along, 0)

    outgoing, accum, probe_part = lax.fori_loop(
        0, wave_count + depth_count - 1, backward_step, (empty_wave, accum_start, probe_start)
    )
    spill_rows = accum[:, :, tile_rows:, :]
    arrived = from_behind(spill_rows, "scan", 1)
    object_grad = accum[:, :, :tile_rows, :].at[:, :, :window_width, :].add(arrived)
    scan_total = lax.psum(probe_part, "scan")
    spread = broadcast(scan_total, "depth", 0)
    probe_grad = lax.dynamic_slice_in_dim(spread, row_start, probe_rows, 1)
    return (object_grad, probe_grad)


def solution(mesh):
    in_specs = (P("depth", None, "scan", None), P(), P("scan"), P("scan"), P("scan", None, None))
    out_specs = (P("depth", None, "scan", None), P(None, "depth", None))
    return jax.shard_map(body, mesh=mesh, in_specs=in_specs, out_specs=out_specs, check_vma=False)
```

profile of v0, /device:TPU:1, one launch (start us, length us, event | category | flops | bytes accessed | tf_op | source)
XLA Modules:
  0.0 1413.6 jit_solution(2726983441275395307)
XLA Ops:
  7.2 11.7 collective-permute-start.2
  20.2 15.2 %collective-permute-done.2 = f32[3,2,128,256]{3,2,1,0:T(8,128)S(1)} collective-permute-done((f32[3,2,128,256]{3,2,1,0:T(8,128)}, f32[3,2,128,256]{3,2,1,0:T(8,128)S(1)}, u32[]{:S(2)}, u32[]{:S(2)}) %collective-permute-start.2) | collective-permute-done | bytes 786464 | tf_op jit(solution)/shard_map/ppermute | solution.py:14
  36.3 180.3 %while.44 = (s32[]{:T(128)}, f32[2,128,128]{2,1,0:T(8,128)}, f32[2,3,2,128,128]{4,3,2,1,0:T(8,128)S(1)}, f32[2,2,128,128]{3,2,1,0:T(8,128)S(1)}, s32[]{:T(128)},...) while((s32[]{:T(128)}, f32[2,128,128]{2,1,0:T(8,128)}, ...), condition=%wide.region_3.4_spmd.clone.clone.clone, body=%wide.region_0.3_spmd.clone.clone.clone.sunk | while | flops 1209778176 | bytes 16319556 | solution.py:156
  36.3 10.2 collective-permute-start
  63.6 20.9 %conditional.12 = (f32[2,128,128]{2,1,0:T(8,128)}, f32[2,3,2,128,128]{4,3,2,1,0:T(8,128)S(1)}, f32[2,2,128,128]{3,2,1,0:T(8,128)S(1)}) conditional(s32[]{:T(128)} %convert_element_type.355, (f32[2,3,2,128,128]{4,3,2,1,0:T(8,128)S(1)}, f32[2,2,128,128]{3,2,1,0:T(8,128)S(1)}) %tuple.295, (pred[]{:T(512)}, f32[2,128,128]{2,1,0:T(8,128)S(1)}, ...), branch_computations={%region_1.1_spmd, %region_2.2_spmd.clone} | conditional | flops 1209499648 | bytes 15597781 | solution.py:154
  88.7 20.9 %conditional.12 = (f32[2,128,128]{2,1,0:T(8,128)}, f32[2,3,2,128,128]{4,3,2,1,0:T(8,128)S(1)}, f32[2,2,128,128]{3,2,1,0:T(8,128)S(1)}) conditional(s32[]{:T(128)} %convert_element_type.355, (f32[2,3,2,128,128]{4,3,2,1,0:T(8,128)S(1)}, f32[2,2,128,128]{3,2,1,0:T(8,128)S(1)}) %tuple.295, (pred[]{:T(512)}, f32[2,128,128]{2,1,0:T(8,128)S(1)}, ...), branch_computations={%region_1.1_spmd, %region_2.2_spmd.clone} | conditional | flops 1209499648 | bytes 15597781 | solution.py:154
  120.9 28.5 %collective-permute-start = (f32[2,128,128]{2,1,0:T(8,128)}, f32[2,128,128]{2,1,0:T(8,128)S(1)}, u32[]{:S(2)}, u32[]{:S(2)}) collective-permute-start(f32[2,128,128]{2,1,0:T(8,128)} %get-tuple-element.2222), channel_id=1, source_target_pairs={{0,64},{64,128},{128,192},{192,256},{256,320},{320,384},{384,448},... | collective-permute-start | bytes 393224 | tf_op jit(solution)/shard_map/while/body/eval_jaxpr/ppermute | solution.py:20
  163.4 14.2 %collective-permute-start = (f32[2,128,128]{2,1,0:T(8,128)}, f32[2,128,128]{2,1,0:T(8,128)S(1)}, u32[]{:S(2)}, u32[]{:S(2)}) collective-permute-start(f32[2,128,128]{2,1,0:T(8,128)} %get-tuple-element.2222), channel_id=1, source_target_pairs={{0,64},{64,128},{128,192},{192,256},{256,320},{320,384},{384,448},... | collective-permute-start | bytes 393224 | tf_op jit(solution)/shard_map/while/body/eval_jaxpr/ppermute | solution.py:20
  191.5 22.2 %collective-permute-start = (f32[2,128,128]{2,1,0:T(8,128)}, f32[2,128,128]{2,1,0:T(8,128)S(1)}, u32[]{:S(2)}, u32[]{:S(2)}) collective-permute-start(f32[2,128,128]{2,1,0:T(8,128)} %get-tuple-element.2222), channel_id=1, source_target_pairs={{0,64},{64,128},{128,192},{192,256},{256,320},{320,384},{384,448},... | collective-permute-start | bytes 393224 | tf_op jit(solution)/shard_map/while/body/eval_jaxpr/ppermute | solution.py:20
  218.6 396.1 %while.45 = (s32[]{:T(128)}, f32[2,128,128]{2,1,0:T(8,128)}, f32[3,2,256,256]{3,2,1,0:T(8,128)S(1)}, f32[2,128,128]{2,1,0:T(8,128)S(1)}, s32[]{:T(128)}, /*index...) while((s32[]{:T(128)}, f32[2,128,128]{2,1,0:T(8,128)}, ...), condition=%wide.region_9.10_spmd.clone.clone.clone, body=%wide.region_4.9_spmd.clone.clone.clone.sunk | while | flops 1613299712 | bytes 24380844 | solution.py:190
  220.9 10.7 collective-permute-done.1
  234.9 13.5 collective-permute-done.1
  251.7 8.7 collective-permute-done.1
  263.8 22.9 %collective-permute-done.1 = f32[2,128,128]{2,1,0:T(8,128)S(1)} collective-permute-done((f32[2,128,128]{2,1,0:T(8,128)}, f32[2,128,128]{2,1,0:T(8,128)S(1)}, u32[]{:S(2)}, u32[]{:S(2)}) %collective-permute-start.1) | collective-permute-done | bytes 131104 | tf_op jit(solution)/shard_map/while/body/eval_jaxpr/ppermute | solution.py:20
  290.1 8.6 collective-permute-done.1
  302.0 13.8 collective-permute-done.1
  319.2 206.2 %collective-permute-done.1 = f32[2,128,128]{2,1,0:T(8,128)S(1)} collective-permute-done((f32[2,128,128]{2,1,0:T(8,128)}, f32[2,128,128]{2,1,0:T(8,128)S(1)}, u32[]{:S(2)}, u32[]{:S(2)}) %collective-permute-start.1) | collective-permute-done | bytes 131104 | tf_op jit(solution)/shard_map/while/body/eval_jaxpr/ppermute | solution.py:20
  526.0 34.3 %conditional.13 = (f32[2,128,128]{2,1,0:T(8,128)}, f32[3,2,256,256]{3,2,1,0:T(8,128)S(1)}, f32[2,128,128]{2,1,0:T(8,128)S(1)}) conditional(s32[]{:T(128)} %convert_element_type.357, (f32[3,2,256,256]{3,2,1,0:T(8,128)S(1)}, f32[2,128,128]{2,1,0:T(8,128)S(1)}) %tuple.299, (s32[]{:T(128)}, s32[2]{0:T(128)S(1)}, s32[2]{0:T(128)S(1)}, ...), branch_computations={%region_5.5_spmd, %region_6.8_spmd.clone} | conditional | flops 1613021184 | bytes 23134704 | solution.py:188
  551.1 9.3 dynamic_update_slice.13
  562.4 8.4 collective-permute-done.1
  571.4 31.5 %conditional.13 = (f32[2,128,128]{2,1,0:T(8,128)}, f32[3,2,256,256]{3,2,1,0:T(8,128)S(1)}, f32[2,128,128]{2,1,0:T(8,128)S(1)}) conditional(s32[]{:T(128)} %convert_element_type.357, (f32[3,2,256,256]{3,2,1,0:T(8,128)S(1)}, f32[2,128,128]{2,1,0:T(8,128)S(1)}) %tuple.299, (s32[]{:T(128)}, s32[2]{0:T(128)S(1)}, s32[2]{0:T(128)S(1)}, ...), branch_computations={%region_5.5_spmd, %region_6.8_spmd.clone} | conditional | flops 1613021184 | bytes 23134704 | solution.py:188
  614.7 22.6 %collective-permute-start.3 = (f32[3,2,128,256]{3,2,1,0:T(8,128)S(1)}, f32[3,2,128,256]{3,2,1,0:T(8,128)S(1)}, u32[]{:S(2)}, u32[]{:S(2)}) collective-permute-start(f32[3,2,128,256]{3,2,1,0:T(8,128)S(1)} %slice.116), channel_id=1, source_target_pairs={{63,0},{0,1},{1,2},{2,3},{3,4},{4,5},{5,6},{6,7},{7,8},{8,9},{9,10... | collective-permute-start | bytes 2359304 | tf_op jit(solution)/shard_map/ppermute | solution.py:14
  637.4 649.5 %all-reduce.3.cloned.1.call-done = f32[2,128,128]{2,1,0:T(8,128)} async-done(((f32[2,128,128]{2,1,0:T(8,128)}), f32[2,128,128]{2,1,0:T(8,128)}) %all-reduce.3.cloned.1.call-update) | async-done | bytes 131088 | tf_op jit(solution)/shard_map/psum | solution.py:196
  1287.6 116.8 %all-reduce.5.cloned.1.call-done = f32[2,128,128]{2,1,0:T(8,128)} async-done(((f32[2,128,128]{2,1,0:T(8,128)}), f32[2,128,128]{2,1,0:T(8,128)}) %all-reduce.5.cloned.1.call-update) | async-done | bytes 131088 | tf_op jit(solution)/shard_map/psum | solution.py:25
  (380 shorter events, 199.5 us)
Async XLA Ops:
  7.2 1279.8 %all-reduce.3.cloned.1.call-start = ((), (), s32[]{:S(2)}) async-start(), calls=%async_computation | async-start | bytes 262144 | tf_op jit(solution)/shard_map/psum | solution.py:196
  7.2 28.2 %collective-permute-start.2 = (f32[3,2,128,256]{3,2,1,0:T(8,128)}, f32[3,2,128,256]{3,2,1,0:T(8,128)S(1)}, u32[]{:S(2)}, u32[]{:S(2)}) collective-permute-start(f32[3,2,128,256]{3,2,1,0:T(8,128)} %param.19), channel_id=1, source_target_pairs={{1,0},{2,1},{3,2},{4,3},{5,4},{6,5},{7,6},{8,7},{9,8},{10,9},{11,1... | collective-permute-start | bytes 2359304 | tf_op jit(solution)/shard_map/ppermute | solution.py:14
  20.2 16.1 %copy-start.2 = (f32[2,128,128]{2,1,0:T(8,128)S(1)}, f32[2,128,128]{2,1,0:T(8,128)}, u32[]{:S(2)}) copy-start(f32[2,128,128]{2,1,0:T(8,128)} %param.20) | copy-start | bytes 393220
  36.3 12.5 collective-permute-start
  49.5 14.1 collective-permute-start
  84.6 4.2 collective-permute-start
  109.7 10.5 collective-permute-start
  120.9 30.8 %collective-permute-start = (f32[2,128,128]{2,1,0:T(8,128)}, f32[2,128,128]{2,1,0:T(8,128)S(1)}, u32[]{:S(2)}, u32[]{:S(2)}) collective-permute-start(f32[2,128,128]{2,1,0:T(8,128)} %get-tuple-element.2222), channel_id=1, source_target_pairs={{0,64},{64,128},{128,192},{192,256},{256,320},{320,384},{384,448},... | collective-permute-start | bytes 393224 | tf_op jit(solution)/shard_map/while/body/eval_jaxpr/ppermute | solution.py:20
  152.3 10.4 collective-permute-start
  163.4 16.4 %collective-permute-start = (f32[2,128,128]{2,1,0:T(8,128)}, f32[2,128,128]{2,1,0:T(8,128)S(1)}, u32[]{:S(2)}, u32[]{:S(2)}) collective-permute-start(f32[2,128,128]{2,1,0:T(8,128)} %get-tuple-element.2222), channel_id=1, source_target_pairs={{0,64},{64,128},{128,192},{192,256},{256,320},{320,384},{384,448},... | collective-permute-start | bytes 393224 | tf_op jit(solution)/shard_map/while/body/eval_jaxpr/ppermute | solution.py:20
  180.5 10.4 collective-permute-start
  191.5 24.4 %collective-permute-start = (f32[2,128,128]{2,1,0:T(8,128)}, f32[2,128,128]{2,1,0:T(8,128)S(1)}, u32[]{:S(2)}, u32[]{:S(2)}) collective-permute-start(f32[2,128,128]{2,1,0:T(8,128)} %get-tuple-element.2222), channel_id=1, source_target_pairs={{0,64},{64,128},{128,192},{192,256},{256,320},{320,384},{384,448},... | collective-permute-start | bytes 393224 | tf_op jit(solution)/shard_map/while/body/eval_jaxpr/ppermute | solution.py:20
  218.8 12.7 collective-permute-start.1
  232.9 15.5 %collective-permute-start.1 = (f32[2,128,128]{2,1,0:T(8,128)}, f32[2,128,128]{2,1,0:T(8,128)S(1)}, u32[]{:S(2)}, u32[]{:S(2)}) collective-permute-start(f32[2,128,128]{2,1,0:T(8,128)} %get-tuple-element.2270), channel_id=1, source_target_pairs={{64,0},{128,64},{192,128},{256,192},{320,256},{384,320},{448,384},... | collective-permute-start | bytes 393224 | tf_op jit(solution)/shard_map/while/body/eval_jaxpr/ppermute | solution.py:20
  249.7 10.8 collective-permute-start.1
  261.8 25.0 %collective-permute-start.1 = (f32[2,128,128]{2,1,0:T(8,128)}, f32[2,128,128]{2,1,0:T(8,128)S(1)}, u32[]{:S(2)}, u32[]{:S(2)}) collective-permute-start(f32[2,128,128]{2,1,0:T(8,128)} %get-tuple-element.2270), channel_id=1, source_target_pairs={{64,0},{128,64},{192,128},{256,192},{320,256},{384,320},{448,384},... | collective-permute-start | bytes 393224 | tf_op jit(solution)/shard_map/while/body/eval_jaxpr/ppermute | solution.py:20
  288.1 10.6 collective-permute-start.1
  300.0 15.8 %collective-permute-start.1 = (f32[2,128,128]{2,1,0:T(8,128)}, f32[2,128,128]{2,1,0:T(8,128)S(1)}, u32[]{:S(2)}, u32[]{:S(2)}) collective-permute-start(f32[2,128,128]{2,1,0:T(8,128)} %get-tuple-element.2270), channel_id=1, source_target_pairs={{64,0},{128,64},{192,128},{256,192},{320,256},{384,320},{448,384},... | collective-permute-start | bytes 393224 | tf_op jit(solution)/shard_map/while/body/eval_jaxpr/ppermute | solution.py:20
  317.1 208.2 %collective-permute-start.1 = (f32[2,128,128]{2,1,0:T(8,128)}, f32[2,128,128]{2,1,0:T(8,128)S(1)}, u32[]{:S(2)}, u32[]{:S(2)}) collective-permute-start(f32[2,128,128]{2,1,0:T(8,128)} %get-tuple-element.2270), channel_id=1, source_target_pairs={{64,0},{128,64},{192,128},{256,192},{320,256},{384,320},{448,384},... | collective-permute-start | bytes 393224 | tf_op jit(solution)/shard_map/while/body/eval_jaxpr/ppermute | solution.py:20
  560.4 10.4 collective-permute-start.1
  603.0 10.4 collective-permute-start.1
  614.7 22.7 %copy-start.1 = (f32[2,128,128]{2,1,0:T(8,128)}, f32[2,128,128]{2,1,0:T(8,128)S(1)}, u32[]{:S(2)}) copy-start(f32[2,128,128]{2,1,0:T(8,128)S(1)} %get-tuple-element.1471) | copy-start | bytes 393220
  614.7 791.0 %collective-permute-start.3 = (f32[3,2,128,256]{3,2,1,0:T(8,128)S(1)}, f32[3,2,128,256]{3,2,1,0:T(8,128)S(1)}, u32[]{:S(2)}, u32[]{:S(2)}) collective-permute-start(f32[3,2,128,256]{3,2,1,0:T(8,128)S(1)} %slice.116), channel_id=1, source_target_pairs={{63,0},{0,1},{1,2},{2,3},{3,4},{4,5},{5,6},{6,7},{7,8},{8,9},{9,10... | collective-permute-start | bytes 2359304 | tf_op jit(solution)/shard_map/ppermute | solution.py:14
  637.4 767.0 %all-reduce.5.cloned.1.call-start = ((), (), s32[]{:S(2)}) async-start(), calls=%async_computation.1 | async-start | bytes 262144 | tf_op jit(solution)/shard_map/psum | solution.py:25
  (12 other events, 36.1 us)
Sparse Core Ops, SparseCore 0:
  637.5 649.3 all-reduce.2
  1290.7 113.7 all-reduce.4
where the time goes:
time: 1410 us
  waiting for transfers between devices  1110 us (79%)
  starting transfers between devices  161 us (11%)
  matrix products  58.6 us (4%)
  local copies, waits for them, and re-layouts  44.9 us (3%)
  loops' own time  17.9 us (1%)
  between operations  14.2 us (1%)
    psum x1, waiting for transfers between devices, body(): scan_total = lax.psum(probe_part, 'scan')  649 us
    ppermute x18, waiting for transfers between devices, passed_along(): return lax.ppermute(block, axis, route)  324 us
    ppermute x18, starting transfers between devices, passed_along(): return lax.ppermute(block, axis, route)  127 us
    psum x1, waiting for transfers between devices, broadcast(): return lax.psum(jnp.where(mine, x, jnp.zeros_like(x)), axis)  117 us
    dot_general x192, matrix products, matmul_high(): return jnp.matmul(left_side, right_side, precision=lax.Precision.HIGHEST)  58.6 us
    ppermute x2, starting transfers between devices, from_behind(): return lax.ppermute(block, axis, route)  34.3 us
  transfers between devices with their start and end apart: 22, of which 21 were waited for; matrix products, arithmetic and copies ran while one was open for 0% of the time, Pallas kernels for 0%

commit v1 on v0

v1 whole, which is shorter than its diff:
```python
import jax
import jax.numpy as jnp
import ml_dtypes
import numpy as np
from jax import lax
from jax.experimental import pallas as pl
from jax.experimental.pallas import tpu as pltpu
from jax.sharding import PartitionSpec as P

PROPAGATION = 0.5
F32 = jnp.float32
BF16 = jnp.bfloat16
MESH = pl.DeviceIdType.MESH


def split_table(table):
    high = table.astype(ml_dtypes.bfloat16)
    low = (table - high.astype(np.float64)).astype(ml_dtypes.bfloat16)
    return high, low


def block_tables(matrix):
    real, imag = matrix.real, matrix.imag
    right_high, right_low = split_table(np.block([[real, imag], [-imag, real]]))
    left_high, left_low = split_table(np.block([[real, -imag], [imag, real]]))
    return np.concatenate([right_high, right_high, right_low], 0), left_high, left_low


def transfer_tables(width):
    index = np.arange(width)
    frequency = np.where(index < width // 2, index, index - width).astype(np.float64)
    fourier = np.exp(-2j * np.pi * (np.outer(index, index) % width) / width) / np.sqrt(width)
    chirp = np.exp(-1j * PROPAGATION * np.pi * frequency**2 / width)
    spread = fourier.conj() @ (chirp[:, None] * fourier)
    return block_tables(spread) + block_tables(fourier)


def grid_of(count):
    sides = []
    while count > 1:
        side = 4 if count % 4 == 0 else 2 if count % 2 == 0 else count
        sides.insert(0, side)
        count //= side
    return sides


def split(x):
    high = x.astype(BF16)
    return high, (x - high.astype(F32)).astype(BF16)


def dot(a, b):
    return jnp.dot(a, b, preferred_element_type=F32)


def both_sides(real, imag, right, left_high, left_low):
    width = real.shape[0]
    high, low = split(jnp.concatenate([real, imag], 1))
    mid = dot(jnp.concatenate([high, low, high], 1), right[...])
    high, low = split(jnp.concatenate([mid[:, :width], mid[:, width:]], 0))
    pair = dot(left_high[...], jnp.concatenate([high, low], 1))
    out = pair[:, :width] + pair[:, width:] + dot(left_low[...], high)
    return out[:width], out[width:]


def make_kernel(depth_count, scan_count, slab, width):
    stages = depth_count // 2
    count = 2 * slab
    sides = grid_of(scan_count)

    def kernel(
        scal, objects, probe, intensity, right, left_high, left_low, dft_right, dft_left_high, dft_left_low,
        grad, probe_grad,
        halo_out, pair_out, own_win, halo_win, ext, win, waves, back_in, back, steps, canvas,
        mine, pair_send, pair_in, spill_out, spill_in, seen_out, seen_in, chunks, parts, total, around,
        send_halo, send_pair, send_wave, send_back, send_grad, send_spill, send_seen, send_chunk, send_around,
        recv_halo, recv_pair, recv_wave, recv_back, recv_grad, recv_spill, recv_seen, recv_chunk, recv_around,
    ):
        dep = lax.axis_index("depth")
        me = lax.axis_index("scan")
        stage = dep // 2
        core = dep % 2
        first = stage == 0
        last = stage == stages - 1
        split_core = core == 0
        after = lax.rem(me + 1, scan_count)
        before = lax.rem(me + scan_count - 1, scan_count)
        partner = (dep + 1 - 2 * core, me)
        crew = [((lax.rem(dep + k, depth_count)), me) for k in range(1, depth_count)]
        cliques = []
        stride = scan_count
        for side in sides:
            stride //= side
            place = (me // stride) % side
            cliques.append(
                [(dep, me + (lax.rem(place + k, side) - place) * stride) for k in range(1, side)]
            )
        friends = crew + [(2 * stage + k, near) for near in (after, before) for k in range(2)]
        for clique in cliques:
            friends = friends + clique

        def copy(source, target, send, recv, device):
            return pltpu.make_async_remote_copy(
                src_ref=source, dst_ref=target, send_sem=send, recv_sem=recv,
                device_id=device, device_id_type=MESH,
            )

        barrier = pltpu.get_barrier_semaphore()
        for friend in friends:
            pl.semaphore_signal(barrier, inc=1, device_id=friend, device_id_type=MESH)
        pl.semaphore_wait(barrier, len(friends))

        col_split, row_split, col_whole, col_before, whole_is_second = [scal[k] for k in range(5)]
        col_mine = jnp.where(split_core, col_split, col_whole)
        col_pair = jnp.where(split_core, col_whole, col_split)
        rows = jnp.where(split_core, row_split, 0)

        def halo_copy(k):
            return copy(
                halo_out.at[k], halo_win.at[slab * core + k], send_halo.at[k],
                recv_halo.at[slab * core + k], (2 * stage, before),
            )

        def pair_copy(k):
            return copy(
                pair_out.at[k], own_win.at[slab * core + k], send_pair.at[k], recv_pair.at[k], partner
            )

        def seen_copy():
            return copy(seen_out, seen_in, send_seen, recv_seen, (dep, after))

        def wave_copy():
            return copy(waves.at[count], waves.at[0], send_wave, recv_wave, (dep + 2, me))

        def back_copy():
            return copy(back, back_in, send_back, recv_back, (dep - 2, me))

        def grad_copy(k):
            return copy(pair_send.at[k], pair_in.at[k], send_grad.at[k], recv_grad.at[k], partner)

        def spill_copy(k):
            return copy(
                spill_out.at[k], spill_in.at[k % slab], send_spill.at[k], recv_spill.at[k % slab],
                (2 * stage + k // slab, after),
            )

        def chunk_copy(k):
            target = lax.rem(dep + k, depth_count)
            return copy(
                chunks.at[target], parts.at[core], send_chunk.at[k], recv_chunk.at[core], (target, me)
            )

        def shifted_left(plane, amount):
            return pltpu.roll(plane, lax.rem(2 * width - amount, 2 * width), 1)[:, :width]

        for k in range(slab):
            for part in range(2):
                plane = objects[k, part]
                halo_out[k, part] = shifted_left(plane, col_before)
                pair_out[k, part] = shifted_left(plane, col_pair)
                own_win[slab * core + k, part] = shifted_left(plane, col_mine)
            halo_copy(k).start()
            pair_copy(k).start()

        measured_split = jnp.where(whole_is_second == 1, intensity[0], intensity[1])
        measured_whole = jnp.where(whole_is_second == 1, intensity[1], intensity[0])

        @pl.when(last & (core == 1))
        def _():
            seen_out[...] = measured_whole
            seen_copy().start()

        @pl.when(split_core)
        def _():
            seen_in[...] = measured_split

        ext[...] = jnp.zeros_like(ext)
        canvas[...] = jnp.zeros_like(canvas)

        def gather_window(k):
            @pl.when(k // slab != core)
            def _():
                copy(
                    pair_out.at[k % slab], own_win.at[k], send_pair.at[k % slab],
                    recv_pair.at[k % slab], partner,
                ).wait_recv()

            @pl.when(split_core)
            def _():
                copy(
                    halo_out.at[k % slab], halo_win.at[k], send_halo.at[k % slab],
                    recv_halo.at[k], partner,
                ).wait_recv()
                ext[:, width:] = halo_win[k]

            ext[:, :width] = own_win[k]
            for part in range(2):
                win[k, part] = ext[part, pl.ds(rows, width), :]

        @pl.when(first)
        def _():
            waves[0] = probe[...]

        @pl.when(jnp.logical_not(first))
        def _():
            lax.fori_loop(0, count, lambda k, c: (gather_window(k), c)[1], 0)
            wave_copy().wait_recv()

        def forward(k, carry):
            @pl.when(first)
            def _():
                gather_window(k)

            real, imag = waves[k, 0], waves[k, 1]
            obj_real, obj_imag = win[k, 0], win[k, 1]
            real, imag = both_sides(
                real * obj_real - imag * obj_imag, real * obj_imag + imag * obj_real,
                right, left_high, left_low,
            )
            waves[k + 1, 0] = real
            waves[k + 1, 1] = imag
            return carry

        lax.fori_loop(0, count, forward, 0)

        @pl.when(jnp.logical_not(last))
        def _():
            wave_copy().start()
            copy(back, back_in, send_back, recv_back, partner).wait_recv()
            back[...] = back_in[...]

        @pl.when(last)
        def _():
            @pl.when(core == 1)
            def _():
                seen_copy().wait_recv()

            real, imag = both_sides(
                waves[count, 0], waves[count, 1], dft_right, dft_left_high, dft_left_low
            )
            misfit = 2.0 * (real * real + imag * imag - seen_in[...])
            real, imag = both_sides(
                misfit * real, -(misfit * imag), dft_right, dft_left_high, dft_left_low
            )
            back[0] = real
            back[1] = imag

        def hand_out(k):
            canvas[:, width:2 * width] = steps[k]
            own = [canvas[part, pl.ds(width - rows, width), :] for part in range(2)]
            at = k % slab

            @pl.when(k // slab == core)
            def _():
                for part in range(2):
                    mine[at, part] = own[part]

            @pl.when(k // slab != core)
            def _():
                for part in range(2):
                    pair_send[at, part] = own[part]
                grad_copy(at).start()

            @pl.when(split_core)
            def _():
                for part in range(2):
                    spill_out[k, part] = canvas[part, pl.ds(2 * width - rows, width), :]
                spill_copy(k).start()

        def backward(step, carry):
            k = count - 1 - step
            real, imag = both_sides(back[0], back[1], right, left_high, left_low)
            wave_real, wave_imag = waves[k, 0], waves[k, 1]
            obj_real, obj_imag = win[k, 0], win[k, 1]
            back[0] = obj_real * real - obj_imag * imag
            back[1] = obj_real * imag + obj_imag * real
            steps[k, 0] = wave_real * real - wave_imag * imag
            steps[k, 1] = -(wave_real * imag + wave_imag * real)

            @pl.when(first)
            def _():
                hand_out(k)

            return carry

        lax.fori_loop(0, count, backward, 0)

        @pl.when(jnp.logical_not(first))
        def _():
            back_copy().start()
            lax.fori_loop(0, count, lambda s, c: (hand_out(count - 1 - s), c)[1], 0)

        share = width // depth_count

        @pl.when(first)
        def _():
            for k in range(depth_count):
                chunks[k, 0] = back[0, k * share:(k + 1) * share]
                chunks[k, 1] = -back[1, k * share:(k + 1) * share]
            for k in range(1, depth_count):
                chunk_copy(k).start()
            parts[core] = chunks[dep]
            copy(chunks.at[0], parts.at[1 - core], send_chunk.at[0], recv_chunk.at[1 - core], partner).wait_recv()

        @pl.when(jnp.logical_not(first))
        def _():
            for k in range(2):
                copy(chunks.at[0], parts.at[k], send_chunk.at[0], recv_chunk.at[k], partner).wait_recv()

        value = parts[0] + parts[1]
        base = 0
        for level, clique in enumerate(cliques):
            total[level] = value
            hops = [
                copy(
                    total.at[level], around.at[base + k], send_around.at[base + k],
                    recv_around.at[base + k], device,
                )
                for k, device in enumerate(clique)
            ]
            for hop in hops:
                hop.start()
            for k, hop in enumerate(hops):
                hop.wait_recv()
                value = value + around[base + k]
            base += len(clique)
        probe_grad[...] = value

        blank = jnp.zeros((width, width), F32)

        def shifted_right(plane, amount):
            return pltpu.roll(jnp.concatenate([plane, blank], 1), amount, 1)

        for k in reversed(range(slab)):
            grad_copy(k).wait_recv()
            copy(spill_out.at[k], spill_in.at[k], send_spill.at[k], recv_spill.at[k], partner).wait_recv()
            for part in range(2):
                grad[k, part] = (
                    shifted_right(mine[k, part], col_mine)
                    + shifted_right(pair_in[k, part], col_pair)
                    + shifted_right(spill_in[k, part], col_before)
                )

        for k in range(slab):
            halo_copy(k).wait_send()
            pair_copy(k).wait_send()
            grad_copy(k).wait_send()

        @pl.when(last & (core == 1))
        def _():
            seen_copy().wait_send()

        @pl.when(split_core)
        def _():
            for k in range(count):
                spill_copy(k).wait_send()

        @pl.when(jnp.logical_not(last))
        def _():
            wave_copy().wait_send()

        @pl.when(jnp.logical_not(first))
        def _():
            back_copy().wait_send()

        @pl.when(first)
        def _():
            for k in range(1, depth_count):
                chunk_copy(k).wait_send()

        base = 0
        for level, clique in enumerate(cliques):
            for k, device in enumerate(clique):
                copy(
                    total.at[level], around.at[base + k], send_around.at[base + k],
                    recv_around.at[base + k], device,
                ).wait_send()
            base += len(clique)

    links = sum(side - 1 for side in sides)
    share = width // depth_count
    plane = (2, width, width)
    buffers = [
        (slab,) + plane, (slab,) + plane, (count,) + plane, (count,) + plane, (2, 2 * width, width),
        (count,) + plane, (count + 1,) + plane, plane, plane, (count,) + plane, (2, 3 * width, width),
        (slab,) + plane, (slab,) + plane, (slab,) + plane, (count,) + plane, (slab,) + plane,
        (width, width), (width, width), (depth_count, 2, share, width), (2, 2, share, width),
        (len(sides), 2, share, width), (links, 2, share, width),
    ]
    dma = pltpu.SemaphoreType.DMA
    marks = [
        dma((slab,)), dma((slab,)), dma, dma, dma((slab,)), dma((count,)), dma, dma((depth_count,)), dma((links,)),
        dma((count,)), dma((slab,)), dma, dma, dma((slab,)), dma((slab,)), dma, dma((2,)), dma((links,)),
    ]
    return kernel, [pltpu.VMEM(shape, F32) for shape in buffers] + marks


def body(objects, probe, row_offsets, col_offsets, intensity):
    slab, _, tile_rows, columns = objects.shape
    width = probe.shape[-1]
    depth_count = lax.axis_size("depth")
    scan_count = lax.axis_size("scan")
    me = lax.axis_index("scan")
    local_rows = row_offsets - me * tile_rows
    second = (local_rows[0] != tile_rows).astype(jnp.int32)
    col_whole = jnp.where(second == 1, col_offsets[1], col_offsets[0])
    col_split = jnp.where(second == 1, col_offsets[0], col_offsets[1])
    row_split = jnp.where(second == 1, local_rows[0], local_rows[1])
    route = [(k, (k + 1) % scan_count) for k in range(scan_count)]
    arrived = lax.ppermute(jnp.stack([col_whole, col_split]), "scan", route)
    zero = jnp.zeros((), jnp.int32)
    scalars = jnp.stack([col_split, row_split, arrived[0], arrived[1], second, zero, zero, zero])
    kernel, scratch = make_kernel(depth_count, scan_count, slab, width)
    tables = [jnp.asarray(table) for table in transfer_tables(width)]
    vmem = pl.BlockSpec(memory_space=pltpu.VMEM)
    return pl.pallas_call(
        kernel,
        out_shape=(
            jax.ShapeDtypeStruct(objects.shape, F32),
            jax.ShapeDtypeStruct((2, width // depth_count, width), F32),
        ),
        in_specs=[pl.BlockSpec(memory_space=pltpu.SMEM)] + [vmem] * 9,
        out_specs=(vmem, vmem),
        scratch_shapes=scratch,
        compiler_params=pltpu.CompilerParams(
            collective_id=0, has_side_effects=True, vmem_limit_bytes=48 << 20
        ),
        name="slices",
    )(scalars, objects, probe, intensity, *tables)


def solution(mesh):
    in_specs = (P("depth", None, "scan", None), P(), P("scan"), P("scan"), P("scan", None, None))
    out_specs = (P("depth", None, "scan", None), P(None, "depth", None))
    return jax.shard_map(body, mesh=mesh, in_specs=in_specs, out_specs=out_specs, check_vma=False)
```

time: 1410 us -> 140 us (0.10)
  waiting for transfers between devices: 1110 us -> 7.4 us
  starting transfers between devices: 161 us -> 3.94 us
  Pallas kernels: 0 us -> 110 us
  matrix products: 58.6 us -> 0 us
  local copies, waits for them, and re-layouts: 44.9 us -> 12.6 us
  loops' own time: 17.9 us -> 0 us
    psum x2 -> x0, waiting for transfers between devices: 766 us -> none  [the longest x1 649 us: body(): scan_total = lax.psum(probe_part, 'scan')]
    ppermute x20 -> x1, waiting for transfers between devices: 339 us -> 7.4 us  [body(): arrived = lax.ppermute(jnp.stack([col_whole, col_split]), 'scan', route)]
    ppermute x20 -> x1, starting transfers between devices: 161 us -> 3.94 us  [body(): arrived = lax.ppermute(jnp.stack([col_whole, col_split]), 'scan', route)]
    pallas_call x0 -> x1, Pallas kernels: none -> 110 us  [body(): pl.pallas_call(kernel, out_shape=(jax.ShapeDtypeStruct(objects.shape, F32...]
    dot_general x192 -> x0, matrix products: 58.6 us -> none  [matmul_high(): return jnp.matmul(left_side, right_side, precision=lax.Precision.HIGHEST)]
    another operation x22 -> x0, loops' own time: 17.9 us -> none  [the longest x9 8.65 us: forward_step(): return lax.cond(active_step, forward_run_section, forward_pass_along, 0)]
    dynamic_update_slice x2 -> x0, local copies, waits for them, and re-layouts: 15.9 us -> none  [add_window(): lax.dynamic_update_slice(accum, lax.dynamic_slice(accum, corner, window_s...]
  transfers between devices with their start and end apart: 22 -> 1, of which waited for: 21 -> 1; matrix products, arithmetic and copies ran while one was open for 0% -> 0% of each run, Pallas kernels for 0% -> 0%
where the time goes in v1:
time: 140 us; the launch traced here: 139 us
  Pallas kernels  110 us (79%)
  local copies, waits for them, and re-layouts  12.6 us (9%)
  waiting for transfers between devices  7.4 us (5%)
  between operations  4.99 us (4%)
  starting transfers between devices  3.94 us (3%)
    pallas_call x1, Pallas kernels, body(): pl.pallas_call(kernel, out_shape=(jax.ShapeDtypeStruct(objects.shape, F32...  110 us
    unnamed x24, local copies, waits for them, and re-layouts  11.3 us
    ppermute x1, waiting for transfers between devices, body(): arrived = lax.ppermute(jnp.stack([col_whole, col_split]), 'scan', route)  7.4 us
    ppermute x1, starting transfers between devices, body(): arrived = lax.ppermute(jnp.stack([col_whole, col_split]), 'scan', route)  3.94 us
  transfers between devices with their start and end apart: 1, of which 1 were waited for; matrix products, arithmetic and copies ran while one was open for 0% of the time, Pallas kernels for 0%

profile of v1, /device:TPU:1, one launch (start us, length us, event | category | flops | bytes accessed | tf_op | source)
XLA Modules:
  0.0 138.8 jit_solution(2751873019693982064)
XLA Ops:
  0.6 0.0 copy-start.10
  0.6 0.6 copy-done.10
  1.3 0.6 fusion
  2.5 0.0 copy-start.9
  2.5 0.6 copy-done.9
  3.2 0.6 fusion.1
  6.2 0.1 pad_add_fusion
  6.2 3.9 %collective-permute-start = (s32[2]{0:T(128)S(1)}, s32[2]{0:T(128)S(1)}, u32[]{:S(2)}, u32[]{:S(2)}) collective-permute-start(s32[2]{0:T(128)S(1)} %pad_add_fusion), channel_id=1, source_target_pairs={{0,1},{1,2},{2,3},{3,4},{4,5},{5,6},{6,7},{7,8},{8,9},{9,10},{10,1... | collective-permute-start | bytes 32 | tf_op jit(solution)/shard_map/ppermute | solution.py:410
  11.5 7.4 %collective-permute-done = s32[2]{0:T(128)S(1)} collective-permute-done((s32[2]{0:T(128)S(1)}, s32[2]{0:T(128)S(1)}, u32[]{:S(2)}, u32[]{:S(2)}) %collective-permute-start) | collective-permute-done | bytes 40 | tf_op jit(solution)/shard_map/ppermute | solution.py:410
  18.9 0.1 stack.24.scal
  19.0 0.0 copy-start
  19.0 1.1 copy-done
  20.1 0.0 copy-start.1
  20.1 1.0 copy-done.1
  21.1 1.0 copy-done.2
  22.1 0.9 copy-done.3
  23.0 0.9 copy-done.4
  23.9 0.9 copy-done.5
  24.8 0.9 copy-done.6
  25.7 0.9 copy-done.7
  26.6 0.9 copy-done.8
  27.5 109.8 %slices.1 = (f32[3,2,128,256]{3,2,1,0:T(8,128)S(1)}, f32[2,16,128]{2,1,0:T(8,128)S(1)}) custom-call(s32[8]{0:T(128)S(1)} %stack.24.scal, f32[3,2,128,256]{3,2,1,0:T(8,128)S(1)} %copy-done, f32[2,128,128]{2,1,0:T(8,128)S(1)} %copy-done.3, f32[2,128,128]{2,1,0:T(8,128)S(1)} %copy-done.4, bf16[768,256]{1,0:T(8,128)(2,1)S(1)} %copy-done.2, ...), custom_call_target="tpu_custom_call" | custom-call | tf_op jit(solution)/shard_map/slices/pallas_call | solution.py:416
  137.3 0.9 copy.15
  138.2 0.6 copy.16
  (9 shorter events, 0.0 us)
Async XLA Ops:
  0.6 0.7 copy-start.10
  2.5 0.7 copy-start.9
  6.2 12.6 %collective-permute-start = (s32[2]{0:T(128)S(1)}, s32[2]{0:T(128)S(1)}, u32[]{:S(2)}, u32[]{:S(2)}) collective-permute-start(s32[2]{0:T(128)S(1)} %pad_add_fusion), channel_id=1, source_target_pairs={{0,1},{1,2},{2,3},{3,4},{4,5},{5,6},{6,7},{7,8},{8,9},{9,10},{10,1... | collective-permute-start | bytes 32 | tf_op jit(solution)/shard_map/ppermute | solution.py:410
  19.0 1.1 copy-start
  20.1 1.0 copy-start.1
  21.1 1.0 copy-start.2
  22.1 0.9 copy-start.3
  23.0 0.9 copy-start.4
  23.9 0.9 copy-start.5
  24.8 0.9 copy-start.6
  25.7 0.9 copy-start.7
  26.6 0.9 copy-start.8

commit v2 on v1

--- a/solution.py
+++ b/solution.py
@@ -69,8 +69,17 @@
     sides = grid_of(scan_count)
 
     def kernel(
-        scal, objects, probe, intensity, right, left_high, left_low, dft_right, dft_left_high, dft_left_low,
-        grad, probe_grad,
+        row_hbm, col_hbm, objects_hbm, probe_hbm, intensity_hbm, *rest
+    ):
+        tables_hbm, rest = rest[:6], rest[6:]
+        grad_hbm, probe_grad, *scratch = rest
+        run(row_hbm, col_hbm, objects_hbm, probe_hbm, intensity_hbm, tables_hbm, grad_hbm, probe_grad, *scratch)
+
+    def run(
+        row_hbm, col_hbm, objects_hbm, probe_hbm, intensity_hbm, tables_hbm, grad_hbm, probe_grad,
+        right, left_high, left_low, dft_right, dft_left_high, dft_left_low,
+        objects, probe, intensity, grad, row_off, col_off, note_out, note_in,
+        load_tables, load_objects, load_small, store_grad, send_note, recv_note,
         halo_out, pair_out, own_win, halo_win, ext, win, waves, back_in, back, steps, canvas,
         mine, pair_send, pair_in, spill_out, spill_in, seen_out, seen_in, chunks, parts, total, around,
         send_halo, send_pair, send_wave, send_back, send_grad, send_spill, send_seen, send_chunk, send_around,
@@ -105,15 +114,34 @@
                 device_id=device, device_id_type=MESH,
             )
 
+        def local(source, target, sem):
+            return pltpu.make_async_copy(source, target, sem)
+
         barrier = pltpu.get_barrier_semaphore()
         for friend in friends:
             pl.semaphore_signal(barrier, inc=1, device_id=friend, device_id_type=MESH)
-        pl.semaphore_wait(barrier, len(friends))
-
-        col_split, row_split, col_whole, col_before, whole_is_second = [scal[k] for k in range(5)]
-        col_mine = jnp.where(split_core, col_split, col_whole)
-        col_pair = jnp.where(split_core, col_whole, col_split)
-        rows = jnp.where(split_core, row_split, 0)
+
+        loads = [local(row_hbm, row_off, load_small.at[0]), local(col_hbm, col_off, load_small.at[1])]
+        object_loads = [local(objects_hbm.at[k], objects.at[k], load_objects.at[k]) for k in range(slab)]
+        small_loads = [local(probe_hbm, probe, load_small.at[2]), local(intensity_hbm, intensity, load_small.at[3])]
+        tables = [right, left_high, left_low, dft_right, dft_left_high, dft_left_low]
+        table_loads = [local(tables_hbm[k], tables[k], load_tables.at[k]) for k in range(6)]
+        for load in loads + object_loads + small_loads + table_loads:
+            load.start()
+
+        for load in loads:
+            load.wait()
+        rows_here = [row_off[k] - me * width for k in range(2)]
+        second = rows_here[0] != width
+        col_split = jnp.where(second, col_off[0], col_off[1])
+        col_whole_here = jnp.where(second, col_off[1], col_off[0])
+        row_split = jnp.where(second, rows_here[0], rows_here[1])
+        rows = jnp.where(split_core, jnp.clip(row_split, 0, width), 0)
+        note_out[0] = col_whole_here
+        note_out[1] = col_split
+
+        def note_copy():
+            return copy(note_out, note_in, send_note, recv_note, (dep, after))
 
         def halo_copy(k):
             return copy(
@@ -154,16 +182,57 @@
             return pltpu.roll(plane, lax.rem(2 * width - amount, 2 * width), 1)[:, :width]
 
         for k in range(slab):
+            object_loads[k].wait()
             for part in range(2):
-                plane = objects[k, part]
-                halo_out[k, part] = shifted_left(plane, col_before)
-                pair_out[k, part] = shifted_left(plane, col_pair)
-                own_win[slab * core + k, part] = shifted_left(plane, col_mine)
+                window = shifted_left(objects[k, part], col_split)
+
+                @pl.when(split_core)
+                def _():
+                    own_win[k, part] = window
+
+                @pl.when(jnp.logical_not(split_core))
+                def _():
+                    pair_out[k, part] = window
+
+        pl.semaphore_wait(barrier, len(friends))
+        note_copy().start()
+
+        @pl.when(jnp.logical_not(split_core))
+        def _():
+            for k in range(slab):
+                pair_copy(k).start()
+
+        ext[...] = jnp.zeros_like(ext)
+        canvas[...] = jnp.zeros_like(canvas)
+        note_copy().wait_recv()
+        col_whole = note_in[0]
+        col_before = note_in[1]
+        col_mine = jnp.where(split_core, col_split, col_whole)
+        col_pair = jnp.where(split_core, col_whole, col_split)
+
+        for k in range(slab):
+            for part in range(2):
+                halo_out[k, part] = shifted_left(objects[k, part], col_before)
             halo_copy(k).start()
-            pair_copy(k).start()
-
-        measured_split = jnp.where(whole_is_second == 1, intensity[0], intensity[1])
-        measured_whole = jnp.where(whole_is_second == 1, intensity[1], intensity[0])
+            for part in range(2):
+                window = shifted_left(objects[k, part], col_whole)
+
+                @pl.when(split_core)
+                def _():
+                    pair_out[k, part] = window
+
+                @pl.when(jnp.logical_not(split_core))
+                def _():
+                    own_win[slab + k, part] = window
+
+            @pl.when(split_core)
+            def _():
+                pair_copy(k).start()
+
+        for load in small_loads + table_loads:
+            load.wait()
+        measured_split = jnp.where(second, intensity[0], intensity[1])
+        measured_whole = jnp.where(second, intensity[1], intensity[0])
 
         @pl.when(last & (core == 1))
         def _():
@@ -173,9 +242,6 @@
         @pl.when(split_core)
         def _():
             seen_in[...] = measured_split
-
-        ext[...] = jnp.zeros_like(ext)
-        canvas[...] = jnp.zeros_like(canvas)
 
         def gather_window(k):
             @pl.when(k // slab != core)
@@ -277,7 +343,7 @@
             steps[k, 0] = wave_real * real - wave_imag * imag
             steps[k, 1] = -(wave_real * imag + wave_imag * real)
 
-            @pl.when(first)
+            @pl.when(first & (step < 2))
             def _():
                 hand_out(k)
 
@@ -288,7 +354,6 @@
         @pl.when(jnp.logical_not(first))
         def _():
             back_copy().start()
-            lax.fori_loop(0, count, lambda s, c: (hand_out(count - 1 - s), c)[1], 0)
 
         share = width // depth_count
 
@@ -300,6 +365,13 @@
             for k in range(1, depth_count):
                 chunk_copy(k).start()
             parts[core] = chunks[dep]
+
+        lax.fori_loop(
+            jnp.where(first, 2, 0), count, lambda s, c: (hand_out(count - 1 - s), c)[1], 0
+        )
+
+        @pl.when(first)
+        def _():
             copy(chunks.at[0], parts.at[1 - core], send_chunk.at[0], recv_chunk.at[1 - core], partner).wait_recv()
 
         @pl.when(jnp.logical_not(first))
@@ -340,8 +412,11 @@
                     + shifted_right(pair_in[k, part], col_pair)
                     + shifted_right(spill_in[k, part], col_before)
                 )
-
+            local(grad.at[k], grad_hbm.at[k], store_grad.at[k]).start()
+
+        note_copy().wait_send()
         for k in range(slab):
+            local(grad.at[k], grad_hbm.at[k], store_grad.at[k]).wait()
             halo_copy(k).wait_send()
             pair_copy(k).wait_send()
             grad_copy(k).wait_send()
@@ -392,41 +467,38 @@
         dma((slab,)), dma((slab,)), dma, dma, dma((slab,)), dma((count,)), dma, dma((depth_count,)), dma((links,)),
         dma((count,)), dma((slab,)), dma, dma, dma((slab,)), dma((slab,)), dma, dma((2,)), dma((links,)),
     ]
-    return kernel, [pltpu.VMEM(shape, F32) for shape in buffers] + marks
+    square = (2 * width, 2 * width)
+    tables = [(6 * width, 2 * width), square, square] * 2
+    inputs = [(slab, 2, width, 2 * width), plane, plane, (slab, 2, width, 2 * width)]
+    head = [pltpu.VMEM(shape, BF16) for shape in tables] + [pltpu.VMEM(shape, F32) for shape in inputs]
+    head += [pltpu.SMEM((2,), jnp.int32)] * 4
+    head += [dma((6,)), dma((slab,)), dma((4,)), dma((slab,)), dma, dma]
+    return kernel, head + [pltpu.VMEM(shape, F32) for shape in buffers] + marks
 
 
 def body(objects, probe, row_offsets, col_offsets, intensity):
-    slab, _, tile_rows, columns = objects.shape
+    slab = objects.shape[0]
     width = probe.shape[-1]
     depth_count = lax.axis_size("depth")
     scan_count = lax.axis_size("scan")
-    me = lax.axis_index("scan")
-    local_rows = row_offsets - me * tile_rows
-    second = (local_rows[0] != tile_rows).astype(jnp.int32)
-    col_whole = jnp.where(second == 1, col_offsets[1], col_offsets[0])
-    col_split = jnp.where(second == 1, col_offsets[0], col_offsets[1])
-    row_split = jnp.where(second == 1, local_rows[0], local_rows[1])
-    route = [(k, (k + 1) % scan_count) for k in range(scan_count)]
-    arrived = lax.ppermute(jnp.stack([col_whole, col_split]), "scan", route)
-    zero = jnp.zeros((), jnp.int32)
-    scalars = jnp.stack([col_split, row_split, arrived[0], arrived[1], second, zero, zero, zero])
     kernel, scratch = make_kernel(depth_count, scan_count, slab, width)
     tables = [jnp.asarray(table) for table in transfer_tables(width)]
     vmem = pl.BlockSpec(memory_space=pltpu.VMEM)
+    anywhere = pl.BlockSpec(memory_space=pl.ANY)
     return pl.pallas_call(
         kernel,
         out_shape=(
             jax.ShapeDtypeStruct(objects.shape, F32),
             jax.ShapeDtypeStruct((2, width // depth_count, width), F32),
         ),
-        in_specs=[pl.BlockSpec(memory_space=pltpu.SMEM)] + [vmem] * 9,
-        out_specs=(vmem, vmem),
+        in_specs=[anywhere] * 11,
+        out_specs=(anywhere, vmem),
         scratch_shapes=scratch,
         compiler_params=pltpu.CompilerParams(
-            collective_id=0, has_side_effects=True, vmem_limit_bytes=48 << 20
+            collective_id=0, has_side_effects=True, vmem_limit_bytes=56 << 20
         ),
         name="slices",
-    )(scalars, objects, probe, intensity, *tables)
+    )(row_offsets, col_offsets, objects, probe, intensity, *tables)
 
 
 def solution(mesh):

time: 140 us -> 123 us (0.88)
  local copies, waits for them, and re-layouts: 12.6 us -> 2.71 us
  Pallas kernels: 110 us -> 119 us
  waiting for transfers between devices: 7.4 us -> 0 us
  between operations: 4.99 us -> 0.65 us
  starting transfers between devices: 3.94 us -> 0 us
    pallas_call x1, Pallas kernels: 110 us -> 119 us  [body(): pl.pallas_call(kernel, out_shape=(jax.ShapeDtypeStruct(objects.shape, F32...]
    unnamed x24 -> x4, local copies, waits for them, and re-layouts: 11.3 us -> 2.71 us
    ppermute x1 -> x0, waiting for transfers between devices: 7.4 us -> none  [body(): arrived = lax.ppermute(jnp.stack([col_whole, col_split]), 'scan', route)]
    ppermute x1 -> x0, starting transfers between devices: 3.94 us -> none  [body(): arrived = lax.ppermute(jnp.stack([col_whole, col_split]), 'scan', route)]
  transfers between devices with their start and end apart: 1 -> 0, of which waited for: 1 -> 0; matrix products, arithmetic and copies ran while one was open for 0% -> 0% of each run, Pallas kernels for 0% -> 0%
where the time goes in v2:
time: 123 us; the launch traced here: 122 us
  Pallas kernels  119 us (97%)
  local copies, waits for them, and re-layouts  2.71 us (2%)
    pallas_call x1, Pallas kernels, body(): pl.pallas_call(kernel, out_shape=(jax.ShapeDtypeStruct(objects.shape, F32...  119 us
    unnamed x4, local copies, waits for them, and re-layouts  2.71 us

profile of v2, /device:TPU:1, one launch (start us, length us, event | category | flops | bytes accessed | tf_op | source)
XLA Modules:
  0.0 122.4 jit_solution(5841398832815186517)
XLA Ops:
  0.6 119.0 %slices.1 = (f32[3,2,128,256]{3,2,1,0:T(8,128)}, f32[2,16,128]{2,1,0:T(8,128)}) custom-call(s32[2]{0:T(128)} %row_hbm.1, s32[2]{0:T(128)} %col_hbm.1, f32[3,2,128,256]{3,2,1,0:T(8,128)} %objects_hbm.1, f32[2,128,128]{2,1,0:T(8,128)} %probe_hbm.1, f32[2,128,128]{2,1,0:T(8,128)} %intensity_hbm.1, bf16[768,256]{1,0:T(8,128)(2,1)} %constant.12.clone.rest_0_, ...), custom_call_target="tpu_custom_call" | custom-call | tf_op jit(solution)/shard_map/slices/pallas_call | solution.py:488
  119.7 0.0 copy-start
  119.7 2.1 %copy.15 = f32[3,2,128,256]{3,2,1,0:T(8,128)} copy(f32[3,2,128,256]{3,2,1,0:T(8,128)} %get-tuple-element.4) | data formatting | bytes 1572864
  121.8 0.0 copy-done
  121.8 0.6 copy.16
Async XLA Ops:
  119.7 2.1 %copy-start = (f32[2,16,128]{2,1,0:T(8,128)S(1)}, f32[2,16,128]{2,1,0:T(8,128)}, u32[]{:S(2)}) copy-start(f32[2,16,128]{2,1,0:T(8,128)} %get-tuple-element.5) | copy-start | bytes 49156

commit v3 on v2

--- a/solution.py
+++ b/solution.py
@@ -35,13 +35,8 @@
     return block_tables(spread) + block_tables(fourier)
 
 
-def grid_of(count):
-    sides = []
-    while count > 1:
-        side = 4 if count % 4 == 0 else 2 if count % 2 == 0 else count
-        sides.insert(0, side)
-        count //= side
-    return sides
+def groups_of(count):
+    return [16, count // 16] if count % 16 == 0 and count > 16 else [count]
 
 
 def split(x):
@@ -66,20 +61,22 @@
 def make_kernel(depth_count, scan_count, slab, width):
     stages = depth_count // 2
     count = 2 * slab
-    sides = grid_of(scan_count)
+    sides = groups_of(scan_count)
+    early = min(2, slab)
 
     def kernel(
         row_hbm, col_hbm, objects_hbm, probe_hbm, intensity_hbm, *rest
     ):
         tables_hbm, rest = rest[:6], rest[6:]
-        grad_hbm, probe_grad, *scratch = rest
-        run(row_hbm, col_hbm, objects_hbm, probe_hbm, intensity_hbm, tables_hbm, grad_hbm, probe_grad, *scratch)
+        grad, probe_grad, *scratch = rest
+        run(row_hbm, col_hbm, objects_hbm, probe_hbm, intensity_hbm, tables_hbm, grad, probe_grad, *scratch)
 
     def run(
-        row_hbm, col_hbm, objects_hbm, probe_hbm, intensity_hbm, tables_hbm, grad_hbm, probe_grad,
+        row_hbm, col_hbm, objects_hbm, probe_hbm, intensity_hbm, tables_hbm, grad, probe_grad,
         right, left_high, left_low, dft_right, dft_left_high, dft_left_low,
-        objects, probe, intensity, grad, row_off, col_off, note_out, note_in,
-        load_tables, load_objects, load_small, store_grad, send_note, recv_note,
+        objects, probe, intensity, row_off, col_off, note_out, note_in,
+        load_tables, load_objects, load_small, send_note, recv_note,
+        early_win, far_parts, far_sum, recv_far, send_relay,
         halo_out, pair_out, own_win, halo_win, ext, win, waves, back_in, back, steps, canvas,
         mine, pair_send, pair_in, spill_out, spill_in, seen_out, seen_in, chunks, parts, total, around,
         send_halo, send_pair, send_wave, send_back, send_grad, send_spill, send_seen, send_chunk, send_around,
@@ -95,15 +92,17 @@
         after = lax.rem(me + 1, scan_count)
         before = lax.rem(me + scan_count - 1, scan_count)
         partner = (dep + 1 - 2 * core, me)
-        crew = [((lax.rem(dep + k, depth_count)), me) for k in range(1, depth_count)]
+        ahead = lax.rem(stage + 1, stages)
+        behind = lax.rem(stage + stages - 1, stages)
+        crew = [partner] + [(2 * near + k, me) for near in (ahead, behind) for k in range(2)]
         cliques = []
-        stride = scan_count
+        stride = 1
         for side in sides:
-            stride //= side
             place = (me // stride) % side
             cliques.append(
                 [(dep, me + (lax.rem(place + k, side) - place) * stride) for k in range(1, side)]
             )
+            stride *= side
         friends = crew + [(2 * stage + k, near) for near in (after, before) for k in range(2)]
         for clique in cliques:
             friends = friends + clique
@@ -149,6 +148,11 @@
                 recv_halo.at[slab * core + k], (2 * stage, before),
             )
 
+        def early_copy(k):
+            return copy(
+                objects.at[k], early_win.at[k], send_halo.at[k], recv_halo.at[k], (2 * stage, before)
+            )
+
         def pair_copy(k):
             return copy(
                 pair_out.at[k], own_win.at[slab * core + k], send_pair.at[k], recv_pair.at[k], partner
@@ -172,11 +176,19 @@
                 (2 * stage + k // slab, after),
             )
 
-        def chunk_copy(k):
-            target = lax.rem(dep + k, depth_count)
+        def chunk_copy(target, core_from):
+            if target // 2 == 2 and stages == 4:
+                way = 2 if target % 2 == 0 else 7
+                return copy(
+                    chunks.at[target], far_parts.at[core_from], send_chunk.at[target], recv_far.at[core_from], (way, me)
+                )
             return copy(
-                chunks.at[target], parts.at[core], send_chunk.at[k], recv_chunk.at[core], (target, me)
-            )
+                chunks.at[target], parts.at[core_from], send_chunk.at[target], recv_chunk.at[core_from], (target, me)
+            )
+
+        def relay_copy():
+            target = jnp.where(dep == 2, 4, 5)
+            return copy(far_sum, parts.at[0], send_relay, recv_chunk.at[0], (target, me))
 
         def shifted_left(plane, amount):
             return pltpu.roll(plane, lax.rem(2 * width - amount, 2 * width), 1)[:, :width]
@@ -196,6 +208,11 @@
 
         pl.semaphore_wait(barrier, len(friends))
         note_copy().start()
+
+        @pl.when(split_core)
+        def _():
+            for k in range(early):
+                early_copy(k).start()
 
         @pl.when(jnp.logical_not(split_core))
         def _():
@@ -212,9 +229,6 @@
 
         for k in range(slab):
             for part in range(2):
-                halo_out[k, part] = shifted_left(objects[k, part], col_before)
-            halo_copy(k).start()
-            for part in range(2):
                 window = shifted_left(objects[k, part], col_whole)
 
                 @pl.when(split_core)
@@ -228,6 +242,17 @@
             @pl.when(split_core)
             def _():
                 pair_copy(k).start()
+
+        for k in range(slab):
+            def send_window():
+                for part in range(2):
+                    halo_out[k, part] = shifted_left(objects[k, part], col_before)
+                halo_copy(k).start()
+
+            if k < early:
+                pl.when(jnp.logical_not(split_core))(send_window)
+            else:
+                send_window()
 
         for load in small_loads + table_loads:
             load.wait()
@@ -244,7 +269,7 @@
             seen_in[...] = measured_split
 
         def gather_window(k):
-            @pl.when(k // slab != core)
+            @pl.when(core != k // slab)
             def _():
                 copy(
                     pair_out.at[k % slab], own_win.at[k], send_pair.at[k % slab],
@@ -253,31 +278,22 @@
 
             @pl.when(split_core)
             def _():
-                copy(
-                    halo_out.at[k % slab], halo_win.at[k], send_halo.at[k % slab],
-                    recv_halo.at[k], partner,
-                ).wait_recv()
-                ext[:, width:] = halo_win[k]
+                if k < early:
+                    early_copy(k).wait_recv()
+                    for part in range(2):
+                        ext[part, width:] = shifted_left(early_win[k, part], col_split)
+                else:
+                    copy(
+                        halo_out.at[k % slab], halo_win.at[k], send_halo.at[k % slab],
+                        recv_halo.at[k], partner,
+                    ).wait_recv()
+                    ext[:, width:] = halo_win[k]
 
             ext[:, :width] = own_win[k]
             for part in range(2):
                 win[k, part] = ext[part, pl.ds(rows, width), :]
 
-        @pl.when(first)
-        def _():
-            waves[0] = probe[...]
-
-        @pl.when(jnp.logical_not(first))
-        def _():
-            lax.fori_loop(0, count, lambda k, c: (gather_window(k), c)[1], 0)
-            wave_copy().wait_recv()
-
-        def forward(k, carry):
-            @pl.when(first)
-            def _():
-                gather_window(k)
-
-            real, imag = waves[k, 0], waves[k, 1]
+        def forward(k, real, imag):
             obj_real, obj_imag = win[k, 0], win[k, 1]
             real, imag = both_sides(
                 real * obj_real - imag * obj_imag, real * obj_imag + imag * obj_real,
@@ -285,9 +301,23 @@
             )
             waves[k + 1, 0] = real
             waves[k + 1, 1] = imag
-            return carry
-
-        lax.fori_loop(0, count, forward, 0)
+            return real, imag
+
+        @pl.when(first)
+        def _():
+            waves[0] = probe[...]
+            for k in range(count):
+                gather_window(k)
+                forward(k, waves[k, 0], waves[k, 1])
+
+        @pl.when(jnp.logical_not(first))
+        def _():
+            for k in range(count):
+                gather_window(k)
+            wave_copy().wait_recv()
+            real, imag = waves[0, 0], waves[0, 1]
+            for k in range(count):
+                real, imag = forward(k, real, imag)
 
         @pl.when(jnp.logical_not(last))
         def _():
@@ -333,23 +363,16 @@
                     spill_out[k, part] = canvas[part, pl.ds(2 * width - rows, width), :]
                 spill_copy(k).start()
 
-        def backward(step, carry):
-            k = count - 1 - step
-            real, imag = both_sides(back[0], back[1], right, left_high, left_low)
+        real, imag = back[0], back[1]
+        for k in reversed(range(count)):
+            real, imag = both_sides(real, imag, right, left_high, left_low)
             wave_real, wave_imag = waves[k, 0], waves[k, 1]
             obj_real, obj_imag = win[k, 0], win[k, 1]
-            back[0] = obj_real * real - obj_imag * imag
-            back[1] = obj_real * imag + obj_imag * real
             steps[k, 0] = wave_real * real - wave_imag * imag
             steps[k, 1] = -(wave_real * imag + wave_imag * real)
-
-            @pl.when(first & (step < 2))
-            def _():
-                hand_out(k)
-
-            return carry
-
-        lax.fori_loop(0, count, backward, 0)
+            real, imag = obj_real * real - obj_imag * imag, obj_real * imag + obj_imag * real
+        back[0] = real
+        back[1] = imag
 
         @pl.when(jnp.logical_not(first))
         def _():
@@ -362,22 +385,55 @@
             for k in range(depth_count):
                 chunks[k, 0] = back[0, k * share:(k + 1) * share]
                 chunks[k, 1] = -back[1, k * share:(k + 1) * share]
-            for k in range(1, depth_count):
-                chunk_copy(k).start()
-            parts[core] = chunks[dep]
-
-        lax.fori_loop(
-            jnp.where(first, 2, 0), count, lambda s, c: (hand_out(count - 1 - s), c)[1], 0
-        )
+            for side in range(2):
+                @pl.when(core == side)
+                def _():
+                    for k in range(depth_count):
+                        if k != side:
+                            chunk_copy(k, side).start()
+                    parts[side] = chunks[side]
+
+        lax.fori_loop(0, count, lambda s, c: (hand_out(count - 1 - s), c)[1], 0)
+
+        def await_chunk(k):
+            copy(chunks.at[0], parts.at[k], send_chunk.at[0], recv_chunk.at[k], partner).wait_recv()
+
+        if stages == 4:
+            @pl.when((dep == 2) | (dep == 7))
+            def _():
+                for k in range(2):
+                    copy(chunks.at[0], far_parts.at[k], send_chunk.at[0], recv_far.at[k], partner).wait_recv()
+                far_sum[...] = far_parts[0] + far_parts[1]
+                relay_copy().start()
 
         @pl.when(first)
         def _():
-            copy(chunks.at[0], parts.at[1 - core], send_chunk.at[0], recv_chunk.at[1 - core], partner).wait_recv()
-
-        @pl.when(jnp.logical_not(first))
-        def _():
-            for k in range(2):
-                copy(chunks.at[0], parts.at[k], send_chunk.at[0], recv_chunk.at[k], partner).wait_recv()
+            await_chunk(1 - core)
+
+        @pl.when((stage == 1) | (stage == 3))
+        def _():
+            await_chunk(0)
+            await_chunk(1)
+
+        @pl.when(stage == 2)
+        def _():
+            await_chunk(0)
+            parts[1] = jnp.zeros_like(parts[1])
+
+        blank = jnp.zeros((width, width), F32)
+
+        def shifted_right(plane, amount):
+            return pltpu.roll(jnp.concatenate([plane, blank], 1), amount, 1)
+
+        def add_up(k):
+            grad_copy(k).wait_recv()
+            copy(spill_out.at[k], spill_in.at[k], send_spill.at[k], recv_spill.at[k], partner).wait_recv()
+            for part in range(2):
+                grad[k, part] = (
+                    shifted_right(mine[k, part], col_mine)
+                    + shifted_right(pair_in[k, part], col_pair)
+                    + shifted_right(spill_in[k, part], col_before)
+                )
 
         value = parts[0] + parts[1]
         base = 0
@@ -392,32 +448,22 @@
             ]
             for hop in hops:
                 hop.start()
+            for k in range(slab):
+                if (level == 0) == (k > 0) or len(cliques) == 1:
+                    add_up(k)
             for k, hop in enumerate(hops):
                 hop.wait_recv()
                 value = value + around[base + k]
             base += len(clique)
         probe_grad[...] = value
 
-        blank = jnp.zeros((width, width), F32)
-
-        def shifted_right(plane, amount):
-            return pltpu.roll(jnp.concatenate([plane, blank], 1), amount, 1)
-
-        for k in reversed(range(slab)):
-            grad_copy(k).wait_recv()
-            copy(spill_out.at[k], spill_in.at[k], send_spill.at[k], recv_spill.at[k], partner).wait_recv()
-            for part in range(2):
-                grad[k, part] = (
-                    shifted_right(mine[k, part], col_mine)
-                    + shifted_right(pair_in[k, part], col_pair)
-                    + shifted_right(spill_in[k, part], col_before)
-                )
-            local(grad.at[k], grad_hbm.at[k], store_grad.at[k]).start()
-
         note_copy().wait_send()
         for k in range(slab):
-            local(grad.at[k], grad_hbm.at[k], store_grad.at[k]).wait()
-            halo_copy(k).wait_send()
+            if k < early:
+                pl.when(split_core)(lambda: early_copy(k).wait_send())
+                pl.when(jnp.logical_not(split_core))(lambda: halo_copy(k).wait_send())
+            else:
+                halo_copy(k).wait_send()
             pair_copy(k).wait_send()
             grad_copy(k).wait_send()
 
@@ -440,8 +486,17 @@
 
         @pl.when(first)
         def _():
-            for k in range(1, depth_count):
-                chunk_copy(k).wait_send()
+            for side in range(2):
+                @pl.when(core == side)
+                def _():
+                    for k in range(depth_count):
+                        if k != side:
+                            chunk_copy(k, side).wait_send()
+
+        if stages == 4:
+            @pl.when((dep == 2) | (dep == 7))
+            def _():
+                relay_copy().wait_send()
 
         base = 0
         for level, clique in enumerate(cliques):
@@ -469,10 +524,13 @@
     ]
     square = (2 * width, 2 * width)
     tables = [(6 * width, 2 * width), square, square] * 2
-    inputs = [(slab, 2, width, 2 * width), plane, plane, (slab, 2, width, 2 * width)]
+    inputs = [(slab, 2, width, 2 * width), plane, plane]
     head = [pltpu.VMEM(shape, BF16) for shape in tables] + [pltpu.VMEM(shape, F32) for shape in inputs]
     head += [pltpu.SMEM((2,), jnp.int32)] * 4
-    head += [dma((6,)), dma((slab,)), dma((4,)), dma((slab,)), dma, dma]
+    head += [dma((6,)), dma((slab,)), dma((4,)), dma, dma]
+    piece = (2, share, width)
+    head += [pltpu.VMEM((early, 2, width, 2 * width), F32), pltpu.VMEM((2,) + piece, F32), pltpu.VMEM(piece, F32)]
+    head += [dma((2,)), dma]
     return kernel, head + [pltpu.VMEM(shape, F32) for shape in buffers] + marks
 
 
@@ -492,7 +550,7 @@
             jax.ShapeDtypeStruct((2, width // depth_count, width), F32),
         ),
         in_specs=[anywhere] * 11,
-        out_specs=(anywhere, vmem),
+        out_specs=(vmem, vmem),
         scratch_shapes=scratch,
         compiler_params=pltpu.CompilerParams(
             collective_id=0, has_side_effects=True, vmem_limit_bytes=56 << 20

time: 123 us -> 118 us (0.959)
  the two profiles are of different devices: /device:TPU:1 before, /device:TPU:28 now
where the time goes in v3:
time: 118 us
  Pallas kernels  114 us (97%)
  local copies, waits for them, and re-layouts  2.71 us (2%)
    pallas_call x1, Pallas kernels, body(): pl.pallas_call(kernel, out_shape=(jax.ShapeDtypeStruct(objects.shape, F32...  114 us
    unnamed x4, local copies, waits for them, and re-layouts  2.71 us

profile of v3, /device:TPU:28, one launch (start us, length us, event | category | flops | bytes accessed | tf_op | source)
XLA Modules:
  0.0 117.7 jit_solution(12167317174881435926)
XLA Ops:
  0.6 114.3 %slices.1 = (f32[3,2,128,256]{3,2,1,0:T(8,128)}, f32[2,16,128]{2,1,0:T(8,128)}) custom-call(s32[2]{0:T(128)} %row_hbm.1, s32[2]{0:T(128)} %col_hbm.1, f32[3,2,128,256]{3,2,1,0:T(8,128)} %objects_hbm.1, f32[2,128,128]{2,1,0:T(8,128)} %probe_hbm.1, f32[2,128,128]{2,1,0:T(8,128)} %intensity_hbm.1, bf16[768,256]{1,0:T(8,128)(2,1)} %constant.12.clone.rest_0_, ...), custom_call_target="tpu_custom_call" | custom-call | tf_op jit(solution)/shard_map/slices/pallas_call | solution.py:546
  115.0 0.0 copy-start
  115.0 2.1 %copy.15 = f32[3,2,128,256]{3,2,1,0:T(8,128)} copy(f32[3,2,128,256]{3,2,1,0:T(8,128)} %get-tuple-element.4) | data formatting | bytes 1572864
  117.1 0.0 copy-done
  117.1 0.6 copy.16
Async XLA Ops:
  115.0 2.1 %copy-start = (f32[2,16,128]{2,1,0:T(8,128)S(1)}, f32[2,16,128]{2,1,0:T(8,128)}, u32[]{:S(2)}) copy-start(f32[2,16,128]{2,1,0:T(8,128)} %get-tuple-element.5) | copy-start | bytes 49156

commit v4 on v3

--- a/solution.py
+++ b/solution.py
@@ -62,21 +62,20 @@
     stages = depth_count // 2
     count = 2 * slab
     sides = groups_of(scan_count)
-    early = min(2, slab)
+    early = slab
 
     def kernel(
         row_hbm, col_hbm, objects_hbm, probe_hbm, intensity_hbm, *rest
     ):
         tables_hbm, rest = rest[:6], rest[6:]
-        grad, probe_grad, *scratch = rest
-        run(row_hbm, col_hbm, objects_hbm, probe_hbm, intensity_hbm, tables_hbm, grad, probe_grad, *scratch)
+        run(row_hbm, col_hbm, objects_hbm, probe_hbm, intensity_hbm, tables_hbm, *rest)
 
     def run(
-        row_hbm, col_hbm, objects_hbm, probe_hbm, intensity_hbm, tables_hbm, grad, probe_grad,
+        row_hbm, col_hbm, objects_hbm, probe_hbm, intensity_hbm, tables_hbm, grad, spill_grad, probe_grad, probe_rest,
         right, left_high, left_low, dft_right, dft_left_high, dft_left_low,
         objects, probe, intensity, row_off, col_off, note_out, note_in,
         load_tables, load_objects, load_small, send_note, recv_note,
-        early_win, far_parts, far_sum, recv_far, send_relay,
+        early_win,
         halo_out, pair_out, own_win, halo_win, ext, win, waves, back_in, back, steps, canvas,
         mine, pair_send, pair_in, spill_out, spill_in, seen_out, seen_in, chunks, parts, total, around,
         send_halo, send_pair, send_wave, send_back, send_grad, send_spill, send_seen, send_chunk, send_around,
@@ -88,7 +87,7 @@
         core = dep % 2
         first = stage == 0
         last = stage == stages - 1
-        split_core = core == 0
+        split_core = core == 1
         after = lax.rem(me + 1, scan_count)
         before = lax.rem(me + scan_count - 1, scan_count)
         partner = (dep + 1 - 2 * core, me)
@@ -145,12 +144,12 @@
         def halo_copy(k):
             return copy(
                 halo_out.at[k], halo_win.at[slab * core + k], send_halo.at[k],
-                recv_halo.at[slab * core + k], (2 * stage, before),
+                recv_halo.at[slab * core + k], (2 * stage + 1, before),
             )
 
         def early_copy(k):
             return copy(
-                objects.at[k], early_win.at[k], send_halo.at[k], recv_halo.at[k], (2 * stage, before)
+                objects.at[k], early_win.at[k], send_halo.at[k], recv_halo.at[k], (2 * stage + 1, before)
             )
 
         def pair_copy(k):
@@ -177,18 +176,9 @@
             )
 
         def chunk_copy(target, core_from):
-            if target // 2 == 2 and stages == 4:
-                way = 2 if target % 2 == 0 else 7
-                return copy(
-                    chunks.at[target], far_parts.at[core_from], send_chunk.at[target], recv_far.at[core_from], (way, me)
-                )
             return copy(
                 chunks.at[target], parts.at[core_from], send_chunk.at[target], recv_chunk.at[core_from], (target, me)
             )
-
-        def relay_copy():
-            target = jnp.where(dep == 2, 4, 5)
-            return copy(far_sum, parts.at[0], send_relay, recv_chunk.at[0], (target, me))
 
         def shifted_left(plane, amount):
             return pltpu.roll(plane, lax.rem(2 * width - amount, 2 * width), 1)[:, :width]
@@ -200,7 +190,7 @@
 
                 @pl.when(split_core)
                 def _():
-                    own_win[k, part] = window
+                    own_win[slab + k, part] = window
 
                 @pl.when(jnp.logical_not(split_core))
                 def _():
@@ -209,15 +199,12 @@
         pl.semaphore_wait(barrier, len(friends))
         note_copy().start()
 
-        @pl.when(split_core)
-        def _():
+        @pl.when(core == 0)
+        def _():
+            for k in range(slab):
+                pair_copy(k).start()
             for k in range(early):
                 early_copy(k).start()
-
-        @pl.when(jnp.logical_not(split_core))
-        def _():
-            for k in range(slab):
-                pair_copy(k).start()
 
         ext[...] = jnp.zeros_like(ext)
         canvas[...] = jnp.zeros_like(canvas)
@@ -231,35 +218,31 @@
             for part in range(2):
                 window = shifted_left(objects[k, part], col_whole)
 
-                @pl.when(split_core)
+                @pl.when(core == 0)
+                def _():
+                    own_win[k, part] = window
+
+                @pl.when(core == 1)
                 def _():
                     pair_out[k, part] = window
 
-                @pl.when(jnp.logical_not(split_core))
-                def _():
-                    own_win[slab + k, part] = window
-
-            @pl.when(split_core)
+            @pl.when(core == 1)
             def _():
                 pair_copy(k).start()
 
-        for k in range(slab):
-            def send_window():
+        @pl.when(core == 1)
+        def _():
+            for k in range(slab):
                 for part in range(2):
                     halo_out[k, part] = shifted_left(objects[k, part], col_before)
                 halo_copy(k).start()
-
-            if k < early:
-                pl.when(jnp.logical_not(split_core))(send_window)
-            else:
-                send_window()
 
         for load in small_loads + table_loads:
             load.wait()
         measured_split = jnp.where(second, intensity[0], intensity[1])
         measured_whole = jnp.where(second, intensity[1], intensity[0])
 
-        @pl.when(last & (core == 1))
+        @pl.when(last & (core == 0))
         def _():
             seen_out[...] = measured_whole
             seen_copy().start()
@@ -316,30 +299,42 @@
                 gather_window(k)
             wave_copy().wait_recv()
             real, imag = waves[0, 0], waves[0, 1]
-            for k in range(count):
+            for k in range(count - 1):
                 real, imag = forward(k, real, imag)
+
+            @pl.when(jnp.logical_not(last))
+            def _():
+                forward(count - 1, real, imag)
+
+        def step_back(k, real, imag):
+            wave_real, wave_imag = waves[k, 0], waves[k, 1]
+            obj_real, obj_imag = win[k, 0], win[k, 1]
+            steps[k, 0] = wave_real * real - wave_imag * imag
+            steps[k, 1] = -(wave_real * imag + wave_imag * real)
+            return obj_real * real - obj_imag * imag, obj_real * imag + obj_imag * real
 
         @pl.when(jnp.logical_not(last))
         def _():
             wave_copy().start()
             copy(back, back_in, send_back, recv_back, partner).wait_recv()
-            back[...] = back_in[...]
+            real, imag = both_sides(back_in[0], back_in[1], right, left_high, left_low)
+            back[0], back[1] = step_back(count - 1, real, imag)
 
         @pl.when(last)
         def _():
-            @pl.when(core == 1)
-            def _():
-                seen_copy().wait_recv()
-
+            pl.when(core == 0)(lambda: seen_copy().wait_recv())
+            end = count - 1
+            wave_real, wave_imag = waves[end, 0], waves[end, 1]
+            obj_real, obj_imag = win[end, 0], win[end, 1]
             real, imag = both_sides(
-                waves[count, 0], waves[count, 1], dft_right, dft_left_high, dft_left_low
+                wave_real * obj_real - wave_imag * obj_imag, wave_real * obj_imag + wave_imag * obj_real,
+                dft_right, dft_left_high, dft_left_low,
             )
             misfit = 2.0 * (real * real + imag * imag - seen_in[...])
             real, imag = both_sides(
                 misfit * real, -(misfit * imag), dft_right, dft_left_high, dft_left_low
             )
-            back[0] = real
-            back[1] = imag
+            back[0], back[1] = step_back(end, real, imag)
 
         def hand_out(k):
             canvas[:, width:2 * width] = steps[k]
@@ -364,13 +359,9 @@
                 spill_copy(k).start()
 
         real, imag = back[0], back[1]
-        for k in reversed(range(count)):
+        for k in reversed(range(count - 1)):
             real, imag = both_sides(real, imag, right, left_high, left_low)
-            wave_real, wave_imag = waves[k, 0], waves[k, 1]
-            obj_real, obj_imag = win[k, 0], win[k, 1]
-            steps[k, 0] = wave_real * real - wave_imag * imag
-            steps[k, 1] = -(wave_real * imag + wave_imag * real)
-            real, imag = obj_real * real - obj_imag * imag, obj_real * imag + obj_imag * real
+            real, imag = step_back(k, real, imag)
         back[0] = real
         back[1] = imag
 
@@ -398,27 +389,14 @@
         def await_chunk(k):
             copy(chunks.at[0], parts.at[k], send_chunk.at[0], recv_chunk.at[k], partner).wait_recv()
 
-        if stages == 4:
-            @pl.when((dep == 2) | (dep == 7))
-            def _():
-                for k in range(2):
-                    copy(chunks.at[0], far_parts.at[k], send_chunk.at[0], recv_far.at[k], partner).wait_recv()
-                far_sum[...] = far_parts[0] + far_parts[1]
-                relay_copy().start()
-
         @pl.when(first)
         def _():
             await_chunk(1 - core)
 
-        @pl.when((stage == 1) | (stage == 3))
+        @pl.when(jnp.logical_not(first))
         def _():
             await_chunk(0)
             await_chunk(1)
-
-        @pl.when(stage == 2)
-        def _():
-            await_chunk(0)
-            parts[1] = jnp.zeros_like(parts[1])
 
         blank = jnp.zeros((width, width), F32)
 
@@ -429,11 +407,8 @@
             grad_copy(k).wait_recv()
             copy(spill_out.at[k], spill_in.at[k], send_spill.at[k], recv_spill.at[k], partner).wait_recv()
             for part in range(2):
-                grad[k, part] = (
-                    shifted_right(mine[k, part], col_mine)
-                    + shifted_right(pair_in[k, part], col_pair)
-                    + shifted_right(spill_in[k, part], col_before)
-                )
+                grad[k, part] = shifted_right(mine[k, part], col_mine) + shifted_right(pair_in[k, part], col_pair)
+                spill_grad[k, part] = shifted_right(spill_in[k, part], col_before)
 
         value = parts[0] + parts[1]
         base = 0
@@ -451,23 +426,23 @@
             for k in range(slab):
                 if (level == 0) == (k > 0) or len(cliques) == 1:
                     add_up(k)
+            if level == len(cliques) - 1:
+                probe_grad[...] = value
+                value = jnp.zeros_like(value)
             for k, hop in enumerate(hops):
                 hop.wait_recv()
                 value = value + around[base + k]
             base += len(clique)
-        probe_grad[...] = value
+        probe_rest[...] = value
 
         note_copy().wait_send()
         for k in range(slab):
-            if k < early:
-                pl.when(split_core)(lambda: early_copy(k).wait_send())
-                pl.when(jnp.logical_not(split_core))(lambda: halo_copy(k).wait_send())
-            else:
-                halo_copy(k).wait_send()
+            pl.when(core == 0)(lambda: early_copy(k).wait_send())
+            pl.when(core == 1)(lambda: halo_copy(k).wait_send())
             pair_copy(k).wait_send()
             grad_copy(k).wait_send()
 
-        @pl.when(last & (core == 1))
+        @pl.when(last & (core == 0))
         def _():
             seen_copy().wait_send()
 
@@ -492,11 +467,6 @@
                     for k in range(depth_count):
                         if k != side:
                             chunk_copy(k, side).wait_send()
-
-        if stages == 4:
-            @pl.when((dep == 2) | (dep == 7))
-            def _():
-                relay_copy().wait_send()
 
         base = 0
         for level, clique in enumerate(cliques):
@@ -528,9 +498,7 @@
     head = [pltpu.VMEM(shape, BF16) for shape in tables] + [pltpu.VMEM(shape, F32) for shape in inputs]
     head += [pltpu.SMEM((2,), jnp.int32)] * 4
     head += [dma((6,)), dma((slab,)), dma((4,)), dma, dma]
-    piece = (2, share, width)
-    head += [pltpu.VMEM((early, 2, width, 2 * width), F32), pltpu.VMEM((2,) + piece, F32), pltpu.VMEM(piece, F32)]
-    head += [dma((2,)), dma]
+    head += [pltpu.VMEM((early, 2, width, 2 * width), F32)]
     return kernel, head + [pltpu.VMEM(shape, F32) for shape in buffers] + marks
 
 
@@ -543,20 +511,20 @@
     tables = [jnp.asarray(table) for table in transfer_tables(width)]
     vmem = pl.BlockSpec(memory_space=pltpu.VMEM)
     anywhere = pl.BlockSpec(memory_space=pl.ANY)
-    return pl.pallas_call(
+    share = jax.ShapeDtypeStruct((2, width // depth_count, width), F32)
+    tile = jax.ShapeDtypeStruct(objects.shape, F32)
+    grad, spill_grad, probe_grad, probe_rest = pl.pallas_call(
         kernel,
-        out_shape=(
-            jax.ShapeDtypeStruct(objects.shape, F32),
-            jax.ShapeDtypeStruct((2, width // depth_count, width), F32),
-        ),
+        out_shape=(tile, tile, share, share),
         in_specs=[anywhere] * 11,
-        out_specs=(vmem, vmem),
+        out_specs=(vmem, vmem, vmem, vmem),
         scratch_shapes=scratch,
         compiler_params=pltpu.CompilerParams(
             collective_id=0, has_side_effects=True, vmem_limit_bytes=56 << 20
         ),
         name="slices",
     )(row_offsets, col_offsets, objects, probe, intensity, *tables)
+    return grad + spill_grad, probe_grad + probe_rest
 
 
 def solution(mesh):

time: 118 us -> 126 us (1.068)
  the two profiles are of different devices: /device:TPU:28 before, /device:TPU:32 now
where the time goes in v4:
time: 126 us
  Pallas kernels  121 us (96%)
  other arithmetic  3.7 us (3%)
    pallas_call x1, Pallas kernels, body(): pl.pallas_call(kernel, out_shape=(tile, tile, share, share), in_specs=[an...  121 us
    add x2, other arithmetic, body(): return (grad + spill_grad, probe_grad + probe_rest)  3.7 us

profile of v4, /device:TPU:32, one launch (start us, length us, event | category | flops | bytes accessed | tf_op | source)
XLA Modules:
  0.0 125.7 jit_solution(10575498505128664878)
XLA Ops:
  0.6 121.4 %slices.1 = (f32[3,2,128,256]{3,2,1,0:T(8,128)}, f32[3,2,128,256]{3,2,1,0:T(8,128)}, f32[2,16,128]{2,1,0:T(8,128)}, f32[2,16,128]{2,1,0:T(8,128)}) custom-call(s32[2]{0:T(128)} %row_hbm.1, s32[2]{0:T(128)} %col_hbm.1, f32[3,2,128,256]{3,2,1,0:T(8,128)} %objects_hbm.1, f32[2,128,128]{2,1,0:T(8,128)} %probe_hbm.1, f32[2,128,128]{2,1,0:T(8,128)} %intensity_hbm.1, ...), custom_call_target="tpu_custom_call" | custom-call | tf_op jit(solution)/shard_map/slices/pallas_call | solution.py:516
  122.0 1.3 %add.7 = f32[2,16,128]{2,1,0:T(8,128)} add(f32[2,16,128]{2,1,0:T(8,128)} %get-tuple-element.8, f32[2,16,128]{2,1,0:T(8,128)} %get-tuple-element.9) | non-fusion elementwise | flops 4096 | bytes 49152 | tf_op jit(solution)/shard_map/add | solution.py:527
  123.4 2.4 %add.6 = f32[3,2,128,256]{3,2,1,0:T(8,128)} add(f32[3,2,128,256]{3,2,1,0:T(8,128)} %get-tuple-element.6, f32[3,2,128,256]{3,2,1,0:T(8,128)} %get-tuple-element.7) | non-fusion elementwise | flops 196608 | bytes 2359296 | tf_op jit(solution)/shard_map/add | solution.py:527

commit v5 on v3

--- a/solution.py
+++ b/solution.py
@@ -62,7 +62,7 @@
     stages = depth_count // 2
     count = 2 * slab
     sides = groups_of(scan_count)
-    early = min(2, slab)
+    early = slab
 
     def kernel(
         row_hbm, col_hbm, objects_hbm, probe_hbm, intensity_hbm, *rest
@@ -76,7 +76,7 @@
         right, left_high, left_low, dft_right, dft_left_high, dft_left_low,
         objects, probe, intensity, row_off, col_off, note_out, note_in,
         load_tables, load_objects, load_small, send_note, recv_note,
-        early_win, far_parts, far_sum, recv_far, send_relay,
+        sums, store_sums, early_win, far_parts, far_sum, recv_far, send_relay,
         halo_out, pair_out, own_win, halo_win, ext, win, waves, back_in, back, steps, canvas,
         mine, pair_send, pair_in, spill_out, spill_in, seen_out, seen_in, chunks, parts, total, around,
         send_halo, send_pair, send_wave, send_back, send_grad, send_spill, send_seen, send_chunk, send_around,
@@ -177,7 +177,7 @@
             )
 
         def chunk_copy(target, core_from):
-            if target // 2 == 2 and stages == 4:
+            if False:
                 way = 2 if target % 2 == 0 else 7
                 return copy(
                     chunks.at[target], far_parts.at[core_from], send_chunk.at[target], recv_far.at[core_from], (way, me)
@@ -316,30 +316,42 @@
                 gather_window(k)
             wave_copy().wait_recv()
             real, imag = waves[0, 0], waves[0, 1]
-            for k in range(count):
+            for k in range(count - 1):
                 real, imag = forward(k, real, imag)
+
+            @pl.when(jnp.logical_not(last))
+            def _():
+                forward(count - 1, real, imag)
+
+        def step_back(k, real, imag):
+            wave_real, wave_imag = waves[k, 0], waves[k, 1]
+            obj_real, obj_imag = win[k, 0], win[k, 1]
+            steps[k, 0] = wave_real * real - wave_imag * imag
+            steps[k, 1] = -(wave_real * imag + wave_imag * real)
+            return obj_real * real - obj_imag * imag, obj_real * imag + obj_imag * real
 
         @pl.when(jnp.logical_not(last))
         def _():
             wave_copy().start()
             copy(back, back_in, send_back, recv_back, partner).wait_recv()
-            back[...] = back_in[...]
+            real, imag = both_sides(back_in[0], back_in[1], right, left_high, left_low)
+            back[0], back[1] = step_back(count - 1, real, imag)
 
         @pl.when(last)
         def _():
-            @pl.when(core == 1)
-            def _():
-                seen_copy().wait_recv()
-
+            pl.when(core == 1)(lambda: seen_copy().wait_recv())
+            end = count - 1
+            wave_real, wave_imag = waves[end, 0], waves[end, 1]
+            obj_real, obj_imag = win[end, 0], win[end, 1]
             real, imag = both_sides(
-                waves[count, 0], waves[count, 1], dft_right, dft_left_high, dft_left_low
+                wave_real * obj_real - wave_imag * obj_imag, wave_real * obj_imag + wave_imag * obj_real,
+                dft_right, dft_left_high, dft_left_low,
             )
             misfit = 2.0 * (real * real + imag * imag - seen_in[...])
             real, imag = both_sides(
                 misfit * real, -(misfit * imag), dft_right, dft_left_high, dft_left_low
             )
-            back[0] = real
-            back[1] = imag
+            back[0], back[1] = step_back(end, real, imag)
 
         def hand_out(k):
             canvas[:, width:2 * width] = steps[k]
@@ -364,13 +376,9 @@
                 spill_copy(k).start()
 
         real, imag = back[0], back[1]
-        for k in reversed(range(count)):
+        for k in reversed(range(count - 1)):
             real, imag = both_sides(real, imag, right, left_high, left_low)
-            wave_real, wave_imag = waves[k, 0], waves[k, 1]
-            obj_real, obj_imag = win[k, 0], win[k, 1]
-            steps[k, 0] = wave_real * real - wave_imag * imag
-            steps[k, 1] = -(wave_real * imag + wave_imag * real)
-            real, imag = obj_real * real - obj_imag * imag, obj_real * imag + obj_imag * real
+            real, imag = step_back(k, real, imag)
         back[0] = real
         back[1] = imag
 
@@ -398,7 +406,7 @@
         def await_chunk(k):
             copy(chunks.at[0], parts.at[k], send_chunk.at[0], recv_chunk.at[k], partner).wait_recv()
 
-        if stages == 4:
+        if False:
             @pl.when((dep == 2) | (dep == 7))
             def _():
                 for k in range(2):
@@ -410,15 +418,10 @@
         def _():
             await_chunk(1 - core)
 
-        @pl.when((stage == 1) | (stage == 3))
+        @pl.when(jnp.logical_not(first))
         def _():
             await_chunk(0)
             await_chunk(1)
-
-        @pl.when(stage == 2)
-        def _():
-            await_chunk(0)
-            parts[1] = jnp.zeros_like(parts[1])
 
         blank = jnp.zeros((width, width), F32)
 
@@ -429,11 +432,12 @@
             grad_copy(k).wait_recv()
             copy(spill_out.at[k], spill_in.at[k], send_spill.at[k], recv_spill.at[k], partner).wait_recv()
             for part in range(2):
-                grad[k, part] = (
+                sums[k, part] = (
                     shifted_right(mine[k, part], col_mine)
                     + shifted_right(pair_in[k, part], col_pair)
                     + shifted_right(spill_in[k, part], col_before)
                 )
+            local(sums.at[k], grad.at[k], store_sums.at[k]).start()
 
         value = parts[0] + parts[1]
         base = 0
@@ -459,6 +463,7 @@
 
         note_copy().wait_send()
         for k in range(slab):
+            local(sums.at[k], grad.at[k], store_sums.at[k]).wait()
             if k < early:
                 pl.when(split_core)(lambda: early_copy(k).wait_send())
                 pl.when(jnp.logical_not(split_core))(lambda: halo_copy(k).wait_send())
@@ -493,7 +498,7 @@
                         if k != side:
                             chunk_copy(k, side).wait_send()
 
-        if stages == 4:
+        if False:
             @pl.when((dep == 2) | (dep == 7))
             def _():
                 relay_copy().wait_send()
@@ -529,6 +534,7 @@
     head += [pltpu.SMEM((2,), jnp.int32)] * 4
     head += [dma((6,)), dma((slab,)), dma((4,)), dma, dma]
     piece = (2, share, width)
+    head += [pltpu.VMEM((slab, 2, width, 2 * width), F32), dma((slab,))]
     head += [pltpu.VMEM((early, 2, width, 2 * width), F32), pltpu.VMEM((2,) + piece, F32), pltpu.VMEM(piece, F32)]
     head += [dma((2,)), dma]
     return kernel, head + [pltpu.VMEM(shape, F32) for shape in buffers] + marks
@@ -550,7 +556,7 @@
             jax.ShapeDtypeStruct((2, width // depth_count, width), F32),
         ),
         in_specs=[anywhere] * 11,
-        out_specs=(vmem, vmem),
+        out_specs=(anywhere, vmem),
         scratch_shapes=scratch,
         compiler_params=pltpu.CompilerParams(
             collective_id=0, has_side_effects=True, vmem_limit_bytes=56 << 20

time: 118 us -> 115 us (0.975)
  the two profiles are of different devices: /device:TPU:28 before, /device:TPU:8 now
where the time goes in v5:
time: 115 us
  Pallas kernels  112 us (97%)
  local copies, waits for them, and re-layouts  2.71 us (2%)
    pallas_call x1, Pallas kernels, body(): pl.pallas_call(kernel, out_shape=(jax.ShapeDtypeStruct(objects.shape, F32...  112 us
    unnamed x4, local copies, waits for them, and re-layouts  2.71 us

profile of v5, /device:TPU:8, one launch (start us, length us, event | category | flops | bytes accessed | tf_op | source)
XLA Modules:
  0.0 115.0 jit_solution(13097212958018216524)
XLA Ops:
  0.6 111.6 %slices.1 = (f32[3,2,128,256]{3,2,1,0:T(8,128)}, f32[2,16,128]{2,1,0:T(8,128)}) custom-call(s32[2]{0:T(128)} %row_hbm.1, s32[2]{0:T(128)} %col_hbm.1, f32[3,2,128,256]{3,2,1,0:T(8,128)} %objects_hbm.1, f32[2,128,128]{2,1,0:T(8,128)} %probe_hbm.1, f32[2,128,128]{2,1,0:T(8,128)} %intensity_hbm.1, bf16[768,256]{1,0:T(8,128)(2,1)} %constant.12.clone.rest_0_, ...), custom_call_target="tpu_custom_call" | custom-call | tf_op jit(solution)/shard_map/slices/pallas_call | solution.py:552
  112.3 0.0 copy-start
  112.3 2.1 %copy.15 = f32[3,2,128,256]{3,2,1,0:T(8,128)} copy(f32[3,2,128,256]{3,2,1,0:T(8,128)} %get-tuple-element.4) | data formatting | bytes 1572864
  114.4 0.0 copy-done
  114.4 0.6 copy.16
Async XLA Ops:
  112.3 2.1 %copy-start = (f32[2,16,128]{2,1,0:T(8,128)S(1)}, f32[2,16,128]{2,1,0:T(8,128)}, u32[]{:S(2)}) copy-start(f32[2,16,128]{2,1,0:T(8,128)} %get-tuple-element.5) | copy-start | bytes 49156

commit v6 on v5

--- a/solution.py
+++ b/solution.py
@@ -432,12 +432,11 @@
             grad_copy(k).wait_recv()
             copy(spill_out.at[k], spill_in.at[k], send_spill.at[k], recv_spill.at[k], partner).wait_recv()
             for part in range(2):
-                sums[k, part] = (
+                grad[k, part] = (
                     shifted_right(mine[k, part], col_mine)
                     + shifted_right(pair_in[k, part], col_pair)
                     + shifted_right(spill_in[k, part], col_before)
                 )
-            local(sums.at[k], grad.at[k], store_sums.at[k]).start()
 
         value = parts[0] + parts[1]
         base = 0
@@ -463,7 +462,6 @@
 
         note_copy().wait_send()
         for k in range(slab):
-            local(sums.at[k], grad.at[k], store_sums.at[k]).wait()
             if k < early:
                 pl.when(split_core)(lambda: early_copy(k).wait_send())
                 pl.when(jnp.logical_not(split_core))(lambda: halo_copy(k).wait_send())
@@ -549,14 +547,14 @@
     tables = [jnp.asarray(table) for table in transfer_tables(width)]
     vmem = pl.BlockSpec(memory_space=pltpu.VMEM)
     anywhere = pl.BlockSpec(memory_space=pl.ANY)
-    return pl.pallas_call(
+    held = pl.pallas_call(
         kernel,
         out_shape=(
-            jax.ShapeDtypeStruct(objects.shape, F32),
-            jax.ShapeDtypeStruct((2, width // depth_count, width), F32),
+            pltpu.VMEM(objects.shape, F32),
+            pltpu.VMEM((2, width // depth_count, width), F32),
         ),
         in_specs=[anywhere] * 11,
-        out_specs=(anywhere, vmem),
+        out_specs=(vmem, vmem),
         scratch_shapes=scratch,
         compiler_params=pltpu.CompilerParams(
             collective_id=0, has_side_effects=True, vmem_limit_bytes=56 << 20
@@ -564,6 +562,24 @@
         name="slices",
     )(row_offsets, col_offsets, objects, probe, intensity, *tables)
 
+    def store(grad, probe_grad, grad_hbm, probe_grad_hbm, marks):
+        moves = [pltpu.make_async_copy(grad.at[k], grad_hbm.at[k], marks.at[k]) for k in range(slab)]
+        moves.append(pltpu.make_async_copy(probe_grad, probe_grad_hbm, marks.at[slab]))
+        for move in moves:
+            move.start()
+        for move in moves:
+            move.wait()
+
+    return pl.pallas_call(
+        store,
+        out_shape=tuple(jax.ShapeDtypeStruct(part.shape, F32) for part in held),
+        in_specs=[pl.BlockSpec(memory_space=pltpu.VMEM)] * 2,
+        compiler_params=pltpu.CompilerParams(vmem_limit_bytes=1 << 20),
+        out_specs=(anywhere, anywhere),
+        scratch_shapes=[pltpu.SemaphoreType.DMA((slab + 1,))],
+        name="store",
+    )(*held)
+
 
 def solution(mesh):
     in_specs = (P("depth", None, "scan", None), P(), P("scan"), P("scan"), P("scan", None, None))

time: 115 us -> 113 us (0.983)
  local copies, waits for them, and re-layouts: 2.71 us -> 0 us
    unnamed x4 -> x0, local copies, waits for them, and re-layouts: 2.71 us -> none
    pallas_call x1 -> x2, Pallas kernels: 112 us -> 112 us  [the longest x1 111 us: body(): pl.pallas_call(kernel, out_shape=(pltpu.VMEM(objects.shape, F32), pltpu.V...]
where the time goes in v6:
time: 113 us
  Pallas kernels  112 us (99%)
    pallas_call x1, Pallas kernels, body(): pl.pallas_call(kernel, out_shape=(pltpu.VMEM(objects.shape, F32), pltpu.V...  111 us

profile of v6, /device:TPU:8, one launch (start us, length us, event | category | flops | bytes accessed | tf_op | source)
XLA Modules:
  0.0 112.6 jit_solution(18041383136107098467)
XLA Ops:
  0.6 111.0 %slices.1 = (f32[3,2,128,256]{3,2,1,0:T(8,128)S(1)}, f32[2,16,128]{2,1,0:T(8,128)S(1)}) custom-call(s32[2]{0:T(128)} %row_hbm.1, s32[2]{0:T(128)} %col_hbm.1, f32[3,2,128,256]{3,2,1,0:T(8,128)} %objects_hbm.1, f32[2,128,128]{2,1,0:T(8,128)} %probe_hbm.1, f32[2,128,128]{2,1,0:T(8,128)} %intensity_hbm.1, bf16[768,256]{1,0:T(8,128)(2,1)} %constant.12.clone.rest_0_, ...), custom_call_target="tpu_custom_call" | custom-call | tf_op jit(solution)/shard_map/slices/pallas_call | solution.py:550
  111.7 0.9 store.1

commit v7 on v6

--- a/solution.py
+++ b/solution.py
@@ -92,9 +92,8 @@
         after = lax.rem(me + 1, scan_count)
         before = lax.rem(me + scan_count - 1, scan_count)
         partner = (dep + 1 - 2 * core, me)
-        ahead = lax.rem(stage + 1, stages)
         behind = lax.rem(stage + stages - 1, stages)
-        crew = [partner] + [(2 * near + k, me) for near in (ahead, behind) for k in range(2)]
+        crew = [partner, (2 * behind + core, me)]
         cliques = []
         stride = 1
         for side in sides:
@@ -103,6 +102,7 @@
                 [(dep, me + (lax.rem(place + k, side) - place) * stride) for k in range(1, side)]
             )
             stride *= side
+        cliques.reverse()
         friends = crew + [(2 * stage + k, near) for near in (after, before) for k in range(2)]
         for clique in cliques:
             friends = friends + clique
@@ -379,6 +379,8 @@
         for k in reversed(range(count - 1)):
             real, imag = both_sides(real, imag, right, left_high, left_low)
             real, imag = step_back(k, real, imag)
+            if k == count - 3:
+                pl.when(first)(lambda: hand_out(count - 1))
         back[0] = real
         back[1] = imag
 
@@ -396,12 +398,14 @@
             for side in range(2):
                 @pl.when(core == side)
                 def _():
-                    for k in range(depth_count):
+                    for k in sorted(range(depth_count), key=lambda k: -min(k // 2, stages - k // 2)):
                         if k != side:
                             chunk_copy(k, side).start()
                     parts[side] = chunks[side]
 
-        lax.fori_loop(0, count, lambda s, c: (hand_out(count - 1 - s), c)[1], 0)
+        lax.fori_loop(
+            jnp.where(first, 1, 0), count, lambda s, c: (hand_out(count - 1 - s), c)[1], 0
+        )
 
         def await_chunk(k):
             copy(chunks.at[0], parts.at[k], send_chunk.at[0], recv_chunk.at[k], partner).wait_recv()

time: 113 us -> 110 us (0.973)
  the two profiles are of different devices: /device:TPU:8 before, /device:TPU:1 now
where the time goes in v7:
time: 110 us; the launch traced here: 109 us
  Pallas kernels  108 us (98%)
    pallas_call x1, Pallas kernels, body(): pl.pallas_call(kernel, out_shape=(pltpu.VMEM(objects.shape, F32), pltpu.V...  107 us

profile of v7, /device:TPU:1, one launch (start us, length us, event | category | flops | bytes accessed | tf_op | source)
XLA Modules:
  0.0 108.7 jit_solution(14880803442041956786)
XLA Ops:
  0.6 107.1 %slices.1 = (f32[3,2,128,256]{3,2,1,0:T(8,128)S(1)}, f32[2,16,128]{2,1,0:T(8,128)S(1)}) custom-call(s32[2]{0:T(128)} %row_hbm.1, s32[2]{0:T(128)} %col_hbm.1, f32[3,2,128,256]{3,2,1,0:T(8,128)} %objects_hbm.1, f32[2,128,128]{2,1,0:T(8,128)} %probe_hbm.1, f32[2,128,128]{2,1,0:T(8,128)} %intensity_hbm.1, bf16[768,256]{1,0:T(8,128)(2,1)} %constant.12.clone.rest_0_, ...), custom_call_target="tpu_custom_call" | custom-call | tf_op jit(solution)/shard_map/slices/pallas_call | solution.py:554
  107.7 0.9 store.1

commit v8 on v7

--- a/solution.py
+++ b/solution.py
@@ -98,9 +98,14 @@
         stride = 1
         for side in sides:
             place = (me // stride) % side
-            cliques.append(
-                [(dep, me + (lax.rem(place + k, side) - place) * stride) for k in range(1, side)]
-            )
+            if side == 16:
+                across, along = place % 4, place // 4
+                moves = [(k % 4, k // 4) for k in range(1, 16)]
+                moves.sort(key=lambda move: -min(move[0], 4 - move[0]) - min(move[1], 4 - move[1]))
+                peers = [lax.rem(along + q, 4) * 4 + lax.rem(across + p, 4) for p, q in moves]
+            else:
+                peers = [lax.rem(place + k, side) for k in range(1, side)]
+            cliques.append([(dep, me + (peer - place) * stride) for peer in peers])
             stride *= side
         cliques.reverse()
         friends = crew + [(2 * stage + k, near) for near in (after, before) for k in range(2)]
@@ -456,7 +461,7 @@
             for hop in hops:
                 hop.start()
             for k in range(slab):
-                if (level == 0) == (k > 0) or len(cliques) == 1:
+                if level == len(cliques) - 1:
                     add_up(k)
             for k, hop in enumerate(hops):
                 hop.wait_recv()

time: 110 us -> 110 us (level)
  no operation moved by 1% of the time
where the time goes in v8:
time: 110 us; the launch traced here: 109 us
  Pallas kernels  108 us (98%)
    pallas_call x1, Pallas kernels, body(): pl.pallas_call(kernel, out_shape=(pltpu.VMEM(objects.shape, F32), pltpu.V...  107 us

profile of v8, /device:TPU:1, one launch (start us, length us, event | category | flops | bytes accessed | tf_op | source)
XLA Modules:
  0.0 108.5 jit_solution(18047832337190941815)
XLA Ops:
  0.6 107.0 %slices.1 = (f32[3,2,128,256]{3,2,1,0:T(8,128)S(1)}, f32[2,16,128]{2,1,0:T(8,128)S(1)}) custom-call(s32[2]{0:T(128)} %row_hbm.1, s32[2]{0:T(128)} %col_hbm.1, f32[3,2,128,256]{3,2,1,0:T(8,128)} %objects_hbm.1, f32[2,128,128]{2,1,0:T(8,128)} %probe_hbm.1, f32[2,128,128]{2,1,0:T(8,128)} %intensity_hbm.1, bf16[768,256]{1,0:T(8,128)(2,1)} %constant.12.clone.rest_0_, ...), custom_call_target="tpu_custom_call" | custom-call | tf_op jit(solution)/shard_map/slices/pallas_call | solution.py:559
  107.6 0.9 store.1

commit v9 on v8

--- a/solution.py
+++ b/solution.py
@@ -108,7 +108,7 @@
             cliques.append([(dep, me + (peer - place) * stride) for peer in peers])
             stride *= side
         cliques.reverse()
-        friends = crew + [(2 * stage + k, near) for near in (after, before) for k in range(2)]
+        friends = crew + [(dep, before)]
         for clique in cliques:
             friends = friends + clique
 
@@ -124,6 +124,11 @@
         barrier = pltpu.get_barrier_semaphore()
         for friend in friends:
             pl.semaphore_signal(barrier, inc=1, device_id=friend, device_id_type=MESH)
+
+        @pl.when(core == 0)
+        def _():
+            for k in range(2):
+                pl.semaphore_signal(barrier, inc=1, device_id=(2 * stage + k, after), device_id_type=MESH)
 
         loads = [local(row_hbm, row_off, load_small.at[0]), local(col_hbm, col_off, load_small.at[1])]
         object_loads = [local(objects_hbm.at[k], objects.at[k], load_objects.at[k]) for k in range(slab)]
@@ -211,7 +216,7 @@
                 def _():
                     pair_out[k, part] = window
 
-        pl.semaphore_wait(barrier, len(friends))
+        pl.semaphore_wait(barrier, len(friends) + 1)
         note_copy().start()
 
         @pl.when(split_core)

time: 110 us -> 110 us (level)
  no operation moved by 1% of the time
where the time goes in v9:
time: 110 us; the launch traced here: 109 us
  Pallas kernels  108 us (98%)
    pallas_call x1, Pallas kernels, body(): pl.pallas_call(kernel, out_shape=(pltpu.VMEM(objects.shape, F32), pltpu.V...  107 us

profile of v9, /device:TPU:1, one launch (start us, length us, event | category | flops | bytes accessed | tf_op | source)
XLA Modules:
  0.0 108.6 jit_solution(15141871219971188906)
XLA Ops:
  0.6 107.1 %slices.1 = (f32[3,2,128,256]{3,2,1,0:T(8,128)S(1)}, f32[2,16,128]{2,1,0:T(8,128)S(1)}) custom-call(s32[2]{0:T(128)} %row_hbm.1, s32[2]{0:T(128)} %col_hbm.1, f32[3,2,128,256]{3,2,1,0:T(8,128)} %objects_hbm.1, f32[2,128,128]{2,1,0:T(8,128)} %probe_hbm.1, f32[2,128,128]{2,1,0:T(8,128)} %intensity_hbm.1, bf16[768,256]{1,0:T(8,128)(2,1)} %constant.12.clone.rest_0_, ...), custom_call_target="tpu_custom_call" | custom-call | tf_op jit(solution)/shard_map/slices/pallas_call | solution.py:564
  107.7 0.9 store.1
